TPU v7x, 32 devices: a whole 2x2x4 slice. The times are simulated.
32 devices in a mesh: seg: 4 (over y, x), blk: 8 (over z, core).
Axes of the slice: x: 2, y: 2, z: 4, core: 2. Of those that a mesh axis runs over, the one named last changes fastest.
Arguments:
- state: float32 [32, 4, 16, 2304], P(('seg', 'blk')), may hold values from -6 to 6
- metric: float32 [32, 9, 16, 2304], P(('seg', 'blk')), may hold values from -0.4 to 3, as said below
- block_map: int32 [32], replicated, may hold values from 0 to 31, as said below
- links: int32 [32, 6, 4], replicated, may hold values from -1 to 31, as said below
Outputs:
- advanced: float32 [32, 4, 16, 2304], P(('seg', 'blk'))
Inputs may be any that keep to these rules, and one draw needn't show every extreme that they name: A permutation of the block numbers; device slot d = s * 8 + p (segment s, position p along its chain) holds block block_map[d]. `links`: entries are (partner block or -1, partner face, r_i, r_x). Face 0 of the block at position p > 0 joins face 1 of the block at position p - 1 of the same segment, face 1 at p < 7 joins face 0 at p + 1, both with zero flags; faces 0 at p = 0 and 1 at p = 7 have partner -1. A block has at most one of faces 2 to 5 with a partner, and some blocks have one; that partner lies at the same position p in another segment, names this block and face back with the same flags. Unused fields of a face with partner -1 are 0. `metric`: entries 0, 4 and 8 of the second dimension are positive.
All inputs are finite; a program needn't handle non-finite values.
Results may differ from a plain program's by a relative error of at most 0.0003.
Values sent between devices are 32-bit elements; how exact they have to be, the bound alone decides.
A program may use at most 64 MiB of HBM per device.

v0:
```python
import functools
import math

import jax
import jax.numpy as jnp
from jax import lax
from jax.experimental import pallas as pl
from jax.experimental.pallas import tpu as pltpu
from jax.sharding import PartitionSpec as P

time_step = 0.05
viscosity = 0.2
compress = 1.0
MESH = pl.DeviceIdType.MESH
LANES = 128
WALL = (-1.0, -1.0, -1.0, 1.0)


def split_index(index, size, count):
    quotient = jnp.zeros_like(index)
    for step in range(1, count):
        quotient += (index >= size * step).astype(jnp.int32)
    return quotient, index - size * quotient


def halves(value):
    lead = value.astype(jnp.bfloat16)
    return lead, (value - lead.astype(jnp.float32)).astype(jnp.bfloat16)


def select(flag, yes, no):
    return jnp.where(flag, yes, no)


def kernel(segs, chain, cross, state_hbm, metric_hbm, block_map, links, out_ref,
           first, second, geometry, total, pack_matrix, slope_matrix, bend_matrix,
           split, k_slope_uvw, k_slope_p, k_bend, slope_k, bend_k,
           low_out, high_out, low_in, high_in, face_out, face_in,
           load_sem, chain_send, chain_recv, face_send, face_recv):
    length, width = out_ref.shape[1], out_ref.shape[2]
    chunk = math.lcm(cross, LANES)
    chunks = width // chunk
    inner = pl.ds(LANES, width)
    seg, pos = lax.axis_index("seg"), lax.axis_index("blk")
    me = seg * chain + pos
    has_before, has_after = pos > 0, pos < chain - 1
    before, after = lax.rem(pos + chain - 1, chain), lax.rem(pos + 1, chain)

    load_state = pltpu.make_async_copy(state_hbm.at[0], first.at[:, :, inner], load_sem.at[0])
    load_metric = pltpu.make_async_copy(metric_hbm.at[0], geometry, load_sem.at[1])
    load_state.start()
    load_metric.start()

    barrier = pltpu.get_barrier_semaphore()
    for offset in range(1, segs):
        pl.semaphore_signal(barrier, inc=1, device_id={"seg": lax.rem(seg + offset, segs)}, device_id_type=MESH)

    @pl.when(has_before)
    def _():
        pl.semaphore_signal(barrier, inc=1, device_id={"blk": before}, device_id_type=MESH)

    @pl.when(has_after)
    def _():
        pl.semaphore_signal(barrier, inc=1, device_id={"blk": after}, device_id_type=MESH)

    block = block_map[me]
    joins = [links[2 + side, 0, block] >= 0 for side in range(4)]
    partner, flip_along, flip_across = jnp.int32(-1), jnp.int32(0), jnp.int32(0)
    for side in range(4):
        partner = select(joins[side], links[2 + side, 0, block], partner)
        flip_along = select(joins[side], links[2 + side, 2, block], flip_along)
        flip_across = select(joins[side], links[2 + side, 3, block], flip_across)
    any_join = partner >= 0
    on_first = jnp.logical_or(joins[0], joins[1])
    on_high = jnp.logical_or(joins[1], joins[3])
    own_layers = [select(join, 0.0, 1.0) for join in joins]
    layer_stride = select(on_first, cross, 1)
    cell_stride = select(on_first, 1, cross)
    comes_from = []
    for offset in range(1, segs):
        device = lax.rem(seg + segs - offset, segs) * chain + pos
        comes_from.append(jnp.logical_and(any_join, block_map[device] == partner))

    pads = jnp.zeros((4, length, LANES), jnp.float32)
    for padded in (first, second):
        padded[:, :, :LANES] = pads
        padded[:, :, LANES + width:] = pads

    column = lax.broadcasted_iota(jnp.int32, (1, LANES), 1)
    layer, place = split_index(column, cross, 3)
    layer_place = select(on_high, cross - 1 - layer, layer)
    source = layer_place * layer_stride + place * cell_stride
    source = jnp.where(jnp.logical_and(layer < 2, any_join), source, -1)
    piece = 2 * LANES
    for part in range(width // piece):
        cells = lax.broadcasted_iota(jnp.int32, (piece, LANES), 0) + part * piece
        pack_matrix[part * piece:(part + 1) * piece, :] = (cells == source).astype(jnp.float32).astype(jnp.bfloat16)

    def pack(padded, turn):
        for c in range(4):
            for layer_index in range(2):
                row = 2 * c + layer_index
                low_out[turn, row:row + 1, :] = padded[c, layer_index:layer_index + 1, inner]
                high_out[turn, row:row + 1, :] = padded[c, length - 1 - layer_index:length - layer_index, inner]

    def pack_face(padded, turn):
        rows = 4 * length
        lead, trail = halves(padded[:, :, inner].reshape(rows, width))
        split[0] = lead
        split[1] = trail
        both = jnp.concatenate([lead, trail], axis=0)
        packed = jnp.dot(both, pack_matrix[...], preferred_element_type=jnp.float32)
        face_out[turn] = packed[:rows] + packed[rows:]

    def build_k():
        low, high = own_layers[2], own_layers[3]
        here = lax.broadcasted_iota(jnp.int32, (cross, LANES), 0)
        column = lax.broadcasted_iota(jnp.int32, (cross, LANES), 1)
        for group in range(chunk // cross):
            first_row = group * cross
            for tile in range(chunk // LANES):
                lanes = slice(tile * LANES, (tile + 1) * LANES)
                if not first_row // LANES <= tile <= (first_row + cross - 1) // LANES:
                    for matrix in (k_slope_uvw, k_slope_p, k_bend):
                        for top in (first_row, chunk + first_row):
                            matrix[top:top + cross, lanes] = jnp.zeros((cross, LANES), jnp.bfloat16)
                    continue
                there = column + (tile * LANES - first_row)
                there = jnp.where(jnp.logical_and(there >= 0, there < cross), there, 4 * width)
                offset, mirrored = here - there, here + there

                def at(index, value, factor):
                    return jnp.where(index == value, factor, 0.0)

                slope = at(offset, -2, 1.0) + at(offset, -1, -8.0) + at(offset, 1, 8.0) + at(offset, 2, -1.0)
                bend = (at(offset, -2, -1.0) + at(offset, -1, 16.0) + at(offset, 0, -30.0)
                        + at(offset, 1, 16.0) + at(offset, 2, -1.0))
                end = 2 * cross - 2
                wall_slope = (at(mirrored, 0, -8.0 * low) + at(mirrored, 1, low)
                              + at(mirrored, end, 8.0 * high) + at(mirrored, end - 1, -high))
                wall_bend = (at(mirrored, 0, 16.0 * low) + at(mirrored, 1, -low)
                             + at(mirrored, end, 16.0 * high) + at(mirrored, end - 1, -high))
                for matrix, value in ((k_slope_uvw, slope + WALL[0] * wall_slope),
                                      (k_slope_p, slope + WALL[3] * wall_slope),
                                      (k_bend, bend + WALL[0] * wall_bend)):
                    value = value.astype(jnp.bfloat16)
                    matrix[first_row:first_row + cross, lanes] = value
                    matrix[chunk + first_row:chunk + first_row + cross, lanes] = value

    def along_k():
        rows = 3 * length
        parts = []
        for step in range(chunks):
            at = slice(step * chunk, (step + 1) * chunk)
            parts.append(jnp.concatenate([split[0, :, at], split[1, :, at]], axis=1))
        velocity = jnp.concatenate([part[:rows] for part in parts], axis=0)
        pressure = jnp.concatenate([part[rows:] for part in parts], axis=0)
        slope = jnp.dot(velocity, k_slope_uvw[...], preferred_element_type=jnp.float32)
        bend = jnp.dot(velocity, k_bend[...], preferred_element_type=jnp.float32)
        slope_p = jnp.dot(pressure, k_slope_p[...], preferred_element_type=jnp.float32)
        for step in range(chunks):
            at = slice(step * chunk, (step + 1) * chunk)
            slope_k[:3, :, at] = slope[step * rows:(step + 1) * rows].reshape(3, length, chunk)
            bend_k[:, :, at] = bend[step * rows:(step + 1) * rows].reshape(3, length, chunk)
            slope_k[3, :, at] = slope_p[step * length:(step + 1) * length]

    def chain_copies(turn):
        to_before = pltpu.make_async_remote_copy(
            low_out.at[turn], high_in.at[turn], chain_send.at[turn, 0], chain_recv.at[turn, 0],
            device_id={"blk": before}, device_id_type=MESH)
        to_after = pltpu.make_async_remote_copy(
            high_out.at[turn], low_in.at[turn], chain_send.at[turn, 1], chain_recv.at[turn, 1],
            device_id={"blk": after}, device_id_type=MESH)
        return to_before, to_after

    def face_copies(turn):
        return [pltpu.make_async_remote_copy(
            face_out.at[turn], face_in.at[turn, offset - 1], face_send.at[turn, offset - 1],
            face_recv.at[turn, offset - 1], device_id={"seg": lax.rem(seg + offset, segs)}, device_id_type=MESH)
            for offset in range(1, segs)]

    def start_chain(turn):
        to_before, to_after = chain_copies(turn)

        @pl.when(has_before)
        def _():
            to_before.start()

        @pl.when(has_after)
        def _():
            to_after.start()

    def start_faces(turn):
        for copy in face_copies(turn):
            copy.start()

    def await_chain(turn):
        to_before, to_after = chain_copies(turn)

        @pl.when(has_before)
        def _():
            to_before.wait_send()
            to_after.wait_recv()

        @pl.when(has_after)
        def _():
            to_after.wait_send()
            to_before.wait_recv()

    def await_faces(turn):
        for copy in face_copies(turn):
            copy.wait()

    def build_spread():
        row = lax.broadcasted_iota(jnp.int32, (LANES, 1), 0)
        layer, place = split_index(row, cross, 3)
        place = select(flip_across == 1, cross - 1 - place, place)
        valid = jnp.logical_and(layer < 2, any_join)
        near = select(on_high, cross - 1, 0)
        spot = select(on_high, cross - 2 + layer, 1 - layer)
        outer = jnp.where(valid, spot * layer_stride + place * cell_stride, -1)
        edge = jnp.where(jnp.logical_and(valid, layer == 0), near * layer_stride + place * cell_stride, -1)
        sign = select(on_high, -1.0, 1.0)
        for part in range(width // LANES):
            cells = lax.broadcasted_iota(jnp.int32, (LANES, LANES), 1) + part * LANES
            is_outer = (cells == outer).astype(jnp.float32)
            is_edge = (cells == edge).astype(jnp.float32)
            slope = (sign * (is_outer - 8.0 * is_edge)).astype(jnp.bfloat16)
            bend = (16.0 * is_edge - is_outer).astype(jnp.bfloat16)
            at = slice(part * LANES, (part + 1) * LANES)
            slope_matrix[:LANES, at] = slope
            slope_matrix[LANES:, at] = slope
            bend_matrix[:LANES, at] = bend
            bend_matrix[LANES:, at] = bend

    lane = lax.broadcasted_iota(jnp.int32, (length, chunk), 1)
    row_of = lax.broadcasted_iota(jnp.int32, (length, chunk), 0)

    def central(value, minus2, minus1, plus1, plus2, bent):
        slope = (minus2 - plus2) + 8.0 * (plus1 - minus1)
        if not bent:
            return slope, None
        return slope, 16.0 * (minus1 + plus1) - (minus2 + plus2) - 30.0 * value

    def along(value, bent):
        def moved(step):
            rolled = pltpu.roll(value, step % length, 0)
            inside = row_of >= step if step > 0 else row_of < length + step
            return jnp.where(inside, rolled, 0.0)
        return central(value, moved(2), moved(1), moved(-1), moved(-2), bent)

    def along_j(wide, value, low_factor, high_factor, bent):
        def moved(step):
            if step > 0:
                return pltpu.roll(wide[:, :LANES + chunk], step, 1)[:, LANES:]
            return pltpu.roll(wide[:, LANES:], LANES + chunk + step, 1)[:, :chunk]
        minus2, minus1, plus1, plus2 = moved(2 * cross), moved(cross), moved(-cross), moved(-2 * cross)
        m1, m2, p1, p2 = minus1, minus2, plus1, plus2
        if low_factor is not None:
            m1 = jnp.where(lane < cross, low_factor * value, minus1)
            m2 = jnp.where(lane < cross, low_factor * plus1, jnp.where(lane < 2 * cross, low_factor * minus1, minus2))
        if high_factor is not None:
            p1 = jnp.where(lane >= chunk - cross, high_factor * value, plus1)
            p2 = jnp.where(lane >= chunk - cross, high_factor * minus1,
                           jnp.where(lane >= chunk - 2 * cross, high_factor * plus1, plus2))
        return central(value, m2, m1, p1, p2, bent)

    def weights(metric, values):
        carried = metric[0] * values[0] + metric[1] * values[1] + metric[2] * values[2]
        norm = viscosity * (metric[0] * metric[0] + metric[1] * metric[1] + metric[2] * metric[2])
        return carried, norm

    def rates_of(metric, values, slopes, bends):
        carried, norm = weights(metric, values)
        parts = [norm * bends[c] - carried * slopes[c] - metric[c] * slopes[3] for c in range(3)]
        parts.append(-compress * (metric[0] * slopes[0] + metric[1] * slopes[1] + metric[2] * slopes[2]))
        return parts

    def inside_rates(padded):
        def at_chunk(start, is_first, is_last):
            at = pl.ds(start, chunk)
            wide = [padded[c, :, pl.ds(start, chunk + 2 * LANES)] for c in range(4)]
            values = [w[:, LANES:LANES + chunk] for w in wide]
            sums = None
            for direction in range(3):
                metric = [geometry[3 * direction + b, :, at] for b in range(3)]
                if direction == 2:
                    slopes = [slope_k[c, :, at] for c in range(4)]
                    bends = [bend_k[c, :, at] for c in range(3)]
                else:
                    slopes, bends = [], []
                    for c in range(4):
                        if direction == 0:
                            slope, bend = along(values[c], c < 3)
                        else:
                            low = WALL[c] * own_layers[0] if is_first else None
                            high = WALL[c] * own_layers[1] if is_last else None
                            slope, bend = along_j(wide[c], values[c], low, high, c < 3)
                        slopes.append(slope)
                        bends.append(bend)
                parts = rates_of(metric, values, slopes, bends)
                sums = parts if sums is None else [a + b for a, b in zip(sums, parts)]
            for c in range(4):
                total[c, :, at] = sums[c]

        at_chunk(0, True, chunks == 1)
        if chunks > 2:
            @pl.loop(1, chunks - 1)
            def _(step):
                at_chunk(pl.multiple_of(step * chunk, LANES), False, False)
        if chunks > 1:
            at_chunk((chunks - 1) * chunk, False, True)

    def chain_rates(padded, turn):
        def body(step, carry):
            start = pl.multiple_of(step * chunk, LANES)
            at = pl.ds(start, chunk)
            values = [padded[c, :, pl.ds(pl.multiple_of(start + LANES, LANES), chunk)] for c in range(4)]
            metric = [geometry[b, :, at] for b in range(3)]
            low_own, high_own = low_out[turn, :, at], high_out[turn, :, at]
            low_got, high_got = low_in[turn, :, at], high_in[turn, :, at]
            slopes, bends = [], []
            for c in range(4):
                ghosts = []
                for got, own, there in ((low_got, low_own, has_before), (high_got, high_own, has_after)):
                    for layer_index in range(2):
                        row = 2 * c + layer_index
                        ghosts.append(jnp.where(there, got[row:row + 1], -WALL[c] * own[row:row + 1]))
                low0, low1, high0, high1 = ghosts
                slope = jnp.where(row_of == 0, low1 - 8.0 * low0, 0.0)
                slope = jnp.where(row_of == 1, low0, slope)
                slope = jnp.where(row_of == length - 2, -high0, slope)
                slopes.append(jnp.where(row_of == length - 1, 8.0 * high0 - high1, slope))
                if c < 3:
                    bend = jnp.where(row_of == 0, 16.0 * low0 - low1, 0.0)
                    bend = jnp.where(row_of == 1, -low0, bend)
                    bend = jnp.where(row_of == length - 2, -high0, bend)
                    bends.append(jnp.where(row_of == length - 1, 16.0 * high0 - high1, bend))
            sums = rates_of(metric, values, slopes, bends)
            for c in range(4):
                total[c, :, at] += sums[c]
            return carry

        lax.fori_loop(0, chunks, body, 0)

    def face_rates(padded, turn, finish):
        received = jnp.zeros((4 * length, LANES), jnp.float32)
        for index, here in enumerate(comes_from):
            received = jnp.where(here, face_in[turn, index], received)
        both = jnp.concatenate(halves(received), axis=1)
        target = lax.broadcasted_iota(jnp.int32, (4 * length, 1), 0)
        component, along_index = split_index(target, length, 4)
        along_index = select(flip_along == 1, length - 1 - along_index, along_index)
        target = component * length + along_index
        swap = (lax.broadcasted_iota(jnp.int32, (4 * length, 4 * length), 1) == target)
        swap = swap.astype(jnp.float32).astype(jnp.bfloat16)
        both = jnp.dot(swap, both, preferred_element_type=jnp.float32).astype(jnp.bfloat16)

        def body(step, carry):
            start = pl.multiple_of(step * chunk, LANES)
            at = pl.ds(start, chunk)
            values = [padded[c, :, pl.ds(pl.multiple_of(start + LANES, LANES), chunk)] for c in range(4)]
            metric = [jnp.where(on_first, geometry[3 + b, :, at], geometry[6 + b, :, at]) for b in range(3)]
            slope = jnp.dot(both, slope_matrix[:, at], preferred_element_type=jnp.float32)
            bend = jnp.dot(both[:3 * length], bend_matrix[:, at], preferred_element_type=jnp.float32)
            slopes = [slope[c * length:(c + 1) * length] for c in range(4)]
            bends = [bend[c * length:(c + 1) * length] for c in range(3)]
            parts = rates_of(metric, values, slopes, bends)
            for c in range(4):
                finish(c, start, values[c], total[c, :, at] + parts[c])
            return carry

        lax.fori_loop(0, chunks, body, 0)

    def finish_first(c, start, value, rate):
        second[c, :, pl.ds(pl.multiple_of(start + LANES, LANES), chunk)] = value + (time_step / 12.0) * rate

    def finish_second(c, start, value, rate):
        base = first[c, :, pl.ds(pl.multiple_of(start + LANES, LANES), chunk)]
        out_ref[c, :, pl.ds(start, chunk)] = 0.5 * base + 0.5 * (value + (time_step / 12.0) * rate)

    build_spread()
    build_k()
    load_state.wait()
    pack_face(first, 0)
    pl.semaphore_wait(barrier, segs - 1 + has_before.astype(jnp.int32) + has_after.astype(jnp.int32))

    start_faces(0)
    pack(first, 0)
    start_chain(0)
    along_k()
    load_metric.wait()
    inside_rates(first)
    await_chain(0)
    chain_rates(first, 0)
    await_faces(0)
    face_rates(first, 0, finish_first)

    pack_face(second, 1)
    start_faces(1)
    pack(second, 1)
    start_chain(1)
    along_k()
    inside_rates(second)
    await_chain(1)
    chain_rates(second, 1)
    await_faces(1)
    face_rates(second, 1, finish_second)


def on_device(state, metric, block_map, links):
    segs, chain = lax.axis_size("seg"), lax.axis_size("blk")
    _, parts, length, width = state.shape
    cross = math.isqrt(width)
    chunk = math.lcm(cross, LANES)
    f32, bf16, dma = jnp.float32, jnp.bfloat16, pltpu.SemaphoreType.DMA
    result = pl.pallas_call(
        functools.partial(kernel, segs, chain, cross),
        out_shape=pltpu.VMEM((parts, length, width), f32),
        in_specs=[pl.BlockSpec(memory_space=pl.ANY)] * 2 + [pl.BlockSpec(memory_space=pltpu.SMEM)] * 2,
        out_specs=pl.BlockSpec(memory_space=pltpu.VMEM),
        scratch_shapes=[
            pltpu.VMEM((parts, length, width + 2 * LANES), f32),
            pltpu.VMEM((parts, length, width + 2 * LANES), f32),
            pltpu.VMEM((9, length, width), f32),
            pltpu.VMEM((parts, length, width), f32),
            pltpu.VMEM((width, LANES), bf16),
            pltpu.VMEM((2 * LANES, width), bf16),
            pltpu.VMEM((2 * LANES, width), bf16),
            pltpu.VMEM((2, parts * length, width), bf16),
            pltpu.VMEM((2 * chunk, chunk), bf16),
            pltpu.VMEM((2 * chunk, chunk), bf16),
            pltpu.VMEM((2 * chunk, chunk), bf16),
            pltpu.VMEM((parts, length, width), f32),
            pltpu.VMEM((parts - 1, length, width), f32),
            pltpu.VMEM((2, 2 * parts, width), f32),
            pltpu.VMEM((2, 2 * parts, width), f32),
            pltpu.VMEM((2, 2 * parts, width), f32),
            pltpu.VMEM((2, 2 * parts, width), f32),
            pltpu.VMEM((2, parts * length, LANES), f32),
            pltpu.VMEM((2, segs - 1, parts * length, LANES), f32),
            dma((2,)), dma((2, 2)), dma((2, 2)), dma((2, segs - 1)), dma((2, segs - 1)),
        ],
        compiler_params=pltpu.CompilerParams(collective_id=0, has_side_effects=True),
    )(state, metric, block_map, links.transpose(1, 2, 0))
    return result.reshape(state.shape)


def solution(mesh):
    in_specs = (P(("seg", "blk"), None, None, None), P(("seg", "blk"), None, None, None), P(), P())
    out_specs = P(("seg", "blk"), None, None, None)
    return jax.shard_map(
        on_device, mesh=mesh, in_specs=in_specs, out_specs=out_specs, check_vma=False
    )
```

profile of v0, /device:TPU:1, one launch (start us, length us, event | category | flops | bytes accessed | tf_op | source)
XLA Modules:
  0.0 16.3 jit_solution(2317948554264798960)
XLA Ops:
  0.0 15.5 %shard_map.46 = f32[4,16,2304]{2,1,0:T(8,128)S(1)} custom-call(f32[1,4,16,2304]{3,2,1,0:T(8,128)} %state_hbm.1, f32[1,9,16,2304]{3,2,1,0:T(8,128)} %metric_hbm.1, s32[32]{0:T(128)} %block_map.1, s32[6,4,32]{2,1,0:T(4,128)} %bitcast.3), custom_call_target="tpu_custom_call" | custom-call | tf_op jit(solution)/shard_map/pallas_call | solution.py:417
  15.5 0.8 %copy.6 = f32[1,4,16,2304]{3,2,1,0:T(8,128)} copy(f32[1,4,16,2304]{3,2,1,0:T(8,128)S(1)} %bitcast.2) | data formatting | bytes 1179648
where the time goes:
time: 16.6 us; the launch traced here: 16.3 us
  Pallas kernels  15.5 us (93%)
  local copies, waits for them, and re-layouts  0.82 us (5%)
    pallas_call x1, Pallas kernels, on_device(): pl.pallas_call(functools.partial(kernel, segs, chain, cross), out_shape=p...  15.5 us
    unnamed x1, local copies, waits for them, and re-layouts  0.82 us

commit v1 on v0

v1 whole, which is shorter than its diff:
```python
import functools
import math

import jax
import jax.numpy as jnp
from jax import lax
from jax.experimental import pallas as pl
from jax.experimental.pallas import tpu as pltpu
from jax.sharding import PartitionSpec as P

time_step = 0.05
viscosity = 0.2
compress = 1.0
MESH = pl.DeviceIdType.MESH
LANES = 128
HALF = LANES // 2
WALL = (-1.0, -1.0, -1.0, 1.0)


def split_index(index, size, count):
    quotient = jnp.zeros_like(index)
    for step in range(1, count):
        quotient += (index >= size * step).astype(jnp.int32)
    return quotient, index - size * quotient


def flipped_bits(index, bits):
    bit = 1
    while bit <= bits:
        if bits & bit:
            index = index + bit - 2 * bit * lax.rem(lax.div(index, bit), 2)
        bit *= 2
    return index


def halves(value):
    lead = value.astype(jnp.bfloat16)
    return lead, (value - lead.astype(jnp.float32)).astype(jnp.bfloat16)


def select(flag, yes, no):
    return jnp.where(flag, yes, no)


def ghost_terms(scale, sign, near, metric, values):
    carried = sign * (metric[0] * values[0] + metric[1] * values[1] + metric[2] * values[2])
    norm = viscosity * (metric[0] * metric[0] + metric[1] * metric[1] + metric[2] * metric[2])
    edge = (8.0 * scale) * (2.0 * norm + carried) * near
    outer = scale * (norm + carried)
    return edge, outer, [(scale * sign) * m for m in metric]


def ghost_rates(near, terms, ghosts, moved):
    edge, outer, pull = terms
    eight = 8.0 * near
    slopes = [m - eight * g for g, m in zip(ghosts, moved)]
    parts = [edge * ghosts[c] - outer * moved[c] - pull[c] * slopes[3] for c in range(3)]
    parts.append(-compress * (pull[0] * slopes[0] + pull[1] * slopes[1] + pull[2] * slopes[2]))
    return parts


def kernel(segs, chain, cross, state_hbm, metric_hbm, block_map_hbm, links_hbm, out_ref,
           first, second, geometry, face_matrix, split, k_slope_uvw, k_slope_p, k_bend, slope_k, bend_k,
           row_flip, lane_flip, own_face, own_metric, terms_ref, part_ref,
           ghost_rows, face_out, face_in, block_map, links,
           load_sem, chain_send, chain_recv, face_send, face_recv):
    length, width = out_ref.shape[1], out_ref.shape[2]
    rows = 4 * length
    chunk = math.lcm(cross, LANES)
    chunks = width // chunk
    inner = pl.ds(LANES, width)
    seg, pos = lax.axis_index("seg"), lax.axis_index("blk")
    me = seg * chain + pos
    has_before, has_after = pos > 0, pos < chain - 1
    before, after = lax.rem(pos + chain - 1, chain), lax.rem(pos + 1, chain)
    paired = segs & (segs - 1) == 0
    order = range(segs - 1, 0, -1)

    def to_seg(offset):
        return flipped_bits(seg, offset) if paired else lax.rem(seg + offset, segs)

    def from_seg(offset):
        return flipped_bits(seg, offset) if paired else lax.rem(seg + segs - offset, segs)

    barrier = pltpu.get_barrier_semaphore()
    for offset in order:
        pl.semaphore_signal(barrier, inc=1, device_id={"seg": to_seg(offset)}, device_id_type=MESH)

    @pl.when(has_before)
    def _():
        pl.semaphore_signal(barrier, inc=1, device_id={"blk": before}, device_id_type=MESH)

    @pl.when(has_after)
    def _():
        pl.semaphore_signal(barrier, inc=1, device_id={"blk": after}, device_id_type=MESH)

    load_map = pltpu.make_async_copy(block_map_hbm, block_map, load_sem.at[2])
    load_links = pltpu.make_async_copy(links_hbm, links, load_sem.at[3])
    load_state = pltpu.make_async_copy(state_hbm.at[0], first.at[:, :, inner], load_sem.at[0])
    load_metric = pltpu.make_async_copy(metric_hbm.at[0], geometry, load_sem.at[1])
    load_map.start()
    load_links.start()
    load_state.start()
    load_metric.start()

    lane_row = lax.broadcasted_iota(jnp.int32, (1, LANES), 1)
    face_layer = (lane_row >= HALF).astype(jnp.int32)
    face_place = lane_row - HALF * face_layer
    in_face = face_place < cross
    near_lane = (lane_row < HALF).astype(jnp.float32)

    def build_k():
        here = lax.broadcasted_iota(jnp.int32, (cross, LANES), 0)
        column = lax.broadcasted_iota(jnp.int32, (cross, LANES), 1)
        for group in range(chunk // cross):
            first_row = group * cross
            for tile in range(chunk // LANES):
                lanes = slice(tile * LANES, (tile + 1) * LANES)
                if not first_row // LANES <= tile <= (first_row + cross - 1) // LANES:
                    for matrix in (k_slope_uvw, k_slope_p, k_bend):
                        for top in (first_row, chunk + first_row):
                            matrix[top:top + cross, lanes] = jnp.zeros((cross, LANES), jnp.bfloat16)
                    continue
                there = column + (tile * LANES - first_row)
                there = jnp.where(jnp.logical_and(there >= 0, there < cross), there, 4 * width)
                offset, mirrored = here - there, here + there

                def at(index, value, factor):
                    return jnp.where(index == value, factor, 0.0)

                slope = at(offset, -2, 1.0) + at(offset, -1, -8.0) + at(offset, 1, 8.0) + at(offset, 2, -1.0)
                bend = (at(offset, -2, -1.0) + at(offset, -1, 16.0) + at(offset, 0, -30.0)
                        + at(offset, 1, 16.0) + at(offset, 2, -1.0))
                end = 2 * cross - 2
                wall_slope = (at(mirrored, 0, -8.0) + at(mirrored, 1, 1.0)
                              + at(mirrored, end, 8.0) + at(mirrored, end - 1, -1.0))
                wall_bend = (at(mirrored, 0, 16.0) + at(mirrored, 1, -1.0)
                             + at(mirrored, end, 16.0) + at(mirrored, end - 1, -1.0))
                for matrix, value in ((k_slope_uvw, slope + WALL[0] * wall_slope),
                                      (k_slope_p, slope + WALL[3] * wall_slope),
                                      (k_bend, bend + WALL[0] * wall_bend)):
                    value = value.astype(jnp.bfloat16)
                    matrix[first_row:first_row + cross, lanes] = value
                    matrix[chunk + first_row:chunk + first_row + cross, lanes] = value

    pads = jnp.zeros((4, length, LANES), jnp.float32)
    for padded in (first, second):
        padded[:, :, :LANES] = pads
        padded[:, :, LANES + width:] = pads
    build_k()

    load_map.wait()
    load_links.wait()
    block = block_map[me]
    joins = [links[2 + side, 0, block] >= 0 for side in range(4)]
    partner, flip_along, flip_across = jnp.int32(-1), jnp.int32(0), jnp.int32(0)
    for side in range(4):
        partner = select(joins[side], links[2 + side, 0, block], partner)
        flip_along = select(joins[side], links[2 + side, 2, block], flip_along)
        flip_across = select(joins[side], links[2 + side, 3, block], flip_across)
    any_join = partner >= 0
    on_first = jnp.logical_or(joins[0], joins[1])
    on_second = jnp.logical_or(joins[2], joins[3])
    on_high = jnp.logical_or(joins[1], joins[3])
    comes_from = {offset: block_map[from_seg(offset) * chain + pos] == partner for offset in order}
    face_sign = select(on_high, -1.0, 1.0)

    def build_faces():
        place = jnp.where(in_face, face_place, 0)
        source = place * cross + select(on_high, cross - 1 - face_layer, face_layer)
        source = jnp.where(jnp.logical_and(in_face, on_second), source, -1)
        piece = 2 * LANES
        cells = lax.broadcasted_iota(jnp.int32, (piece, LANES), 0)
        for part in range(width // piece):
            hit = cells == source - part * piece
            face_matrix[part * piece:(part + 1) * piece, :] = hit.astype(jnp.float32).astype(jnp.bfloat16)

    def build_flips():
        target = lax.broadcasted_iota(jnp.int32, (rows, 1), 0)
        component, along_index = split_index(target, length, 4)
        along_index = select(flip_along == 1, length - 1 - along_index, along_index)
        target = component * length + along_index
        hit = lax.broadcasted_iota(jnp.int32, (rows, rows), 1) == target
        row_flip[...] = hit.astype(jnp.float32).astype(jnp.bfloat16)
        place = select(flip_across == 1, cross - 1 - face_place, face_place)
        origin = jnp.where(in_face, face_layer * HALF + place, -1)
        hit = lax.broadcasted_iota(jnp.int32, (LANES, LANES), 0) == origin
        hit = hit.astype(jnp.float32).astype(jnp.bfloat16)
        lane_flip[:LANES, :] = hit
        lane_flip[LANES:, :] = hit

    def flipped(value):
        count = value.shape[0]
        both = jnp.concatenate(halves(value), axis=1)
        both = jnp.dot(row_flip[:count, :count], both, preferred_element_type=jnp.float32)
        return jnp.dot(both.astype(jnp.bfloat16), lane_flip[...], preferred_element_type=jnp.float32)

    def split_up(value):
        count = value.shape[0]
        lead, trail = halves(value)
        split[:count] = lead
        split[count:2 * count] = trail

    def gathered(low, high, count):
        packed = jnp.dot(split[:2 * count], face_matrix[...], preferred_element_type=jnp.float32)
        packed = packed[:count] + packed[count:]
        near, far = LANES - cross, LANES - 2 * cross
        lower = jnp.where(lane_row < HALF, low, pltpu.roll(low, HALF - cross, 1))
        upper = jnp.where(lane_row < HALF, pltpu.roll(high, LANES - near, 1), pltpu.roll(high, HALF - far, 1))
        return jnp.where(on_first, jnp.where(on_high, upper, lower), packed)

    def gather_face(padded):
        low = padded[:, :, LANES:2 * LANES].reshape(rows, LANES)
        high = padded[:, :, width:width + LANES].reshape(rows, LANES)
        return gathered(low, high, rows)

    def spread(value, read, write):
        lead, trail = halves(value)
        both = jnp.concatenate([lead, trail], axis=0)
        near, far = LANES - cross, LANES - 2 * cross
        lower = jnp.where(lane_row < cross, value, pltpu.roll(value, LANES - (HALF - cross), 1))
        lower = jnp.where(jnp.logical_and(lane_row < 2 * cross, jnp.logical_and(on_first, jnp.logical_not(on_high))),
                          lower, 0.0)
        upper = jnp.where(lane_row >= near, pltpu.roll(value, near, 1), pltpu.roll(value, LANES - (HALF - far), 1))
        upper = jnp.where(jnp.logical_and(lane_row >= far, jnp.logical_and(on_first, on_high)), upper, 0.0)
        piece = 2 * LANES
        for part in range(width // piece):
            out = lax.dot_general(both, face_matrix[part * piece:(part + 1) * piece, :],
                                  (((1,), (1,)), ((), ())), preferred_element_type=jnp.float32)
            out = out[:rows] + out[rows:]
            for tile in range(2):
                start = part * piece + tile * LANES
                add = out[:, tile * LANES:(tile + 1) * LANES]
                if start == 0:
                    add = add + lower
                if start == width - LANES:
                    add = add + upper
                for c in range(4):
                    write(c, start, read(c, start) + add[c * length:(c + 1) * length])

    def along_k():
        count = 3 * length
        parts = []
        for step in range(chunks):
            at = slice(step * chunk, (step + 1) * chunk)
            parts.append(jnp.concatenate([split[:rows, at], split[rows:, at]], axis=1))
        velocity = jnp.concatenate([part[:count] for part in parts], axis=0)
        pressure = jnp.concatenate([part[count:] for part in parts], axis=0)
        slope = jnp.dot(velocity, k_slope_uvw[...], preferred_element_type=jnp.float32)
        bend = jnp.dot(velocity, k_bend[...], preferred_element_type=jnp.float32)
        slope_p = jnp.dot(pressure, k_slope_p[...], preferred_element_type=jnp.float32)
        for step in range(chunks):
            at = slice(step * chunk, (step + 1) * chunk)
            slope_k[:3, :, at] = slope[step * count:(step + 1) * count].reshape(3, length, chunk)
            bend_k[:, :, at] = bend[step * count:(step + 1) * count].reshape(3, length, chunk)
            slope_k[3, :, at] = slope_p[step * length:(step + 1) * length]

    def chain_copies(padded, turn):
        to_before = pltpu.make_async_remote_copy(
            padded.at[:, 0:2, inner], ghost_rows.at[turn, :, 6:8], chain_send.at[turn, 0], chain_recv.at[turn, 0],
            device_id={"blk": before}, device_id_type=MESH)
        to_after = pltpu.make_async_remote_copy(
            padded.at[:, length - 2:length, inner], ghost_rows.at[turn, :, 0:2],
            chain_send.at[turn, 1], chain_recv.at[turn, 1], device_id={"blk": after}, device_id_type=MESH)
        return to_before, to_after

    def face_copies(turn):
        return [pltpu.make_async_remote_copy(
            face_out.at[turn], face_in.at[turn, offset - 1], face_send.at[turn, offset - 1],
            face_recv.at[turn, offset - 1], device_id={"seg": to_seg(offset)}, device_id_type=MESH)
            for offset in order]

    def start_chain(padded, turn):
        to_before, to_after = chain_copies(padded, turn)

        @pl.when(has_before)
        def _():
            to_before.start()

        @pl.when(has_after)
        def _():
            to_after.start()

        @pl.when(jnp.logical_not(has_before))
        def _():
            for c in range(4):
                ghost_rows[turn, c, 0:1, :] = -WALL[c] * padded[c, 1:2, inner]
                ghost_rows[turn, c, 1:2, :] = -WALL[c] * padded[c, 0:1, inner]

        @pl.when(jnp.logical_not(has_after))
        def _():
            for c in range(4):
                ghost_rows[turn, c, 6:7, :] = -WALL[c] * padded[c, length - 1:length, inner]
                ghost_rows[turn, c, 7:8, :] = -WALL[c] * padded[c, length - 2:length - 1, inner]

    def await_chain(padded, turn):
        to_before, to_after = chain_copies(padded, turn)

        @pl.when(has_before)
        def _():
            to_after.wait_recv()

        @pl.when(has_after)
        def _():
            to_before.wait_recv()

    def sent_chain(padded, turn):
        to_before, to_after = chain_copies(padded, turn)

        @pl.when(has_before)
        def _():
            to_before.wait_send()

        @pl.when(has_after)
        def _():
            to_after.wait_send()

    lane = lax.broadcasted_iota(jnp.int32, (length, chunk), 1)
    row_of = lax.broadcasted_iota(jnp.int32, (length, chunk), 0)

    def central(value, minus2, minus1, plus1, plus2, bent):
        slope = (minus2 - plus2) + 8.0 * (plus1 - minus1)
        if not bent:
            return slope, None
        return slope, 16.0 * (minus1 + plus1) - (minus2 + plus2) - 30.0 * value

    def along(value, bent):
        def moved(step):
            rolled = pltpu.roll(value, step % length, 0)
            inside = row_of >= step if step > 0 else row_of < length + step
            return jnp.where(inside, rolled, 0.0)
        return central(value, moved(2), moved(1), moved(-1), moved(-2), bent)

    def along_j(wide, value, wall, is_first, is_last, bent):
        def moved(step):
            if step > 0:
                return pltpu.roll(wide[:, :LANES + chunk], step, 1)[:, LANES:]
            return pltpu.roll(wide[:, LANES:], LANES + chunk + step, 1)[:, :chunk]
        minus2, minus1, plus1, plus2 = moved(2 * cross), moved(cross), moved(-cross), moved(-2 * cross)
        m1, m2, p1, p2 = minus1, minus2, plus1, plus2
        if is_first:
            m1 = jnp.where(lane < cross, wall * value, minus1)
            m2 = jnp.where(lane < cross, wall * plus1, jnp.where(lane < 2 * cross, wall * minus1, minus2))
        if is_last:
            p1 = jnp.where(lane >= chunk - cross, wall * value, plus1)
            p2 = jnp.where(lane >= chunk - cross, wall * minus1,
                           jnp.where(lane >= chunk - 2 * cross, wall * plus1, plus2))
        return central(value, m2, m1, p1, p2, bent)

    def rates_of(metric, values, slopes, bends):
        carried = metric[0] * values[0] + metric[1] * values[1] + metric[2] * values[2]
        norm = viscosity * (metric[0] * metric[0] + metric[1] * metric[1] + metric[2] * metric[2])
        parts = [norm * bends[c] - carried * slopes[c] - metric[c] * slopes[3] for c in range(3)]
        parts.append(-compress * (metric[0] * slopes[0] + metric[1] * slopes[1] + metric[2] * slopes[2]))
        return parts

    def inside_rates(padded, finish):
        def at_chunk(start, is_first, is_last):
            at = pl.ds(start, chunk)
            wide = [padded[c, :, pl.ds(start, chunk + 2 * LANES)] for c in range(4)]
            values = [w[:, LANES:LANES + chunk] for w in wide]
            sums = None
            for direction in range(3):
                metric = [geometry[3 * direction + b, :, at] for b in range(3)]
                if direction == 2:
                    slopes = [slope_k[c, :, at] for c in range(4)]
                    bends = [bend_k[c, :, at] for c in range(3)]
                else:
                    slopes, bends = [], []
                    for c in range(4):
                        if direction == 0:
                            slope, bend = along(values[c], c < 3)
                        else:
                            slope, bend = along_j(wide[c], values[c], WALL[c], is_first, is_last, c < 3)
                        slopes.append(slope)
                        bends.append(bend)
                parts = rates_of(metric, values, slopes, bends)
                sums = parts if sums is None else [a + b for a, b in zip(sums, parts)]
            for c in range(4):
                finish(c, start, values[c], sums[c])

        at_chunk(0, True, chunks == 1)
        if chunks > 2:
            @pl.loop(1, chunks - 1)
            def _(step):
                at_chunk(pl.multiple_of(step * chunk, LANES), False, False)
        if chunks > 1:
            at_chunk((chunks - 1) * chunk, False, True)

    sub = lax.broadcasted_iota(jnp.int32, (8, chunk), 0)
    near_row = jnp.where(jnp.logical_or(sub == 0, sub == 7), 1.0, 0.0)
    row_sign = jnp.where(sub < 4, 1.0, -1.0)

    def chain_rates(padded, turn, scale, read, write):
        def body(step, carry):
            start = pl.multiple_of(step * chunk, LANES)
            at = pl.ds(start, chunk)

            def ends(low, high):
                return jnp.where(sub < 4, low, high)

            inside = pl.ds(pl.multiple_of(start + LANES, LANES), chunk)
            values = [ends(padded[c, :8, inside], padded[c, length - 8:, inside]) for c in range(3)]
            metric = [ends(geometry[b, :8, at], geometry[b, length - 8:, at]) for b in range(3)]
            moved = [ghost_rows[turn, c, :, at] for c in range(4)]
            ghosts = [ends(pltpu.roll(m, 7, 0), pltpu.roll(m, 1, 0)) for m in moved]
            sums = ghost_rates(near_row, ghost_terms(scale, row_sign, near_row, metric, values), ghosts, moved)
            for c in range(4):
                write(c, pl.ds(0, 8), start, read(c, pl.ds(0, 8), start) + jnp.where(sub < 2, sums[c], 0.0))
                high = pl.ds(length - 8, 8)
                write(c, high, start, read(c, high, start) + jnp.where(sub >= 6, sums[c], 0.0))
            return carry

        lax.fori_loop(0, chunks, body, 0)

    def at_part(value, c):
        return value[c * length:(c + 1) * length]

    def prepare_terms(scale, metric, own):
        edge, outer, pull = ghost_terms(scale, face_sign, near_lane, [at_part(metric, b) for b in range(3)],
                                        [at_part(own, b) for b in range(3)])
        terms_ref[0] = edge
        terms_ref[1] = outer
        for b in range(3):
            terms_ref[2 + b] = pull[b]

    def face_rates(turn, own):
        received = face_in[turn, order[-1] - 1]
        for offset in order[:-1]:
            received = jnp.where(comes_from[offset], face_in[turn, offset - 1], received)
        ghosts = [at_part(received, c) - WALL[c] * at_part(own, c) for c in range(4)]
        moved = [pltpu.roll(g, HALF, 1) for g in ghosts]
        terms = (terms_ref[0], terms_ref[1], [terms_ref[2 + b] for b in range(3)])
        return jnp.concatenate(ghost_rates(near_lane, terms, ghosts, moved), axis=0)

    def inside_second(start, size):
        return pl.ds(start + LANES if isinstance(start, int) else pl.multiple_of(start + LANES, LANES), size)

    step_one, step_two = time_step / 12.0, 0.5 * time_step / 12.0

    def finish_first(c, start, value, rate):
        second[c, :, inside_second(start, chunk)] = value + step_one * rate

    def finish_second(c, start, value, rate):
        base = first[c, :, inside_second(start, chunk)]
        out_ref[c, :, pl.ds(start, chunk)] = 0.5 * (base + value) + step_two * rate

    def read_second(c, which, start):
        return second[c, which, inside_second(start, chunk)]

    def write_second(c, which, start, value):
        second[c, which, inside_second(start, chunk)] = value

    def read_out(c, which, start):
        return out_ref[c, which, pl.ds(start, chunk)]

    def write_out(c, which, start, value):
        out_ref[c, which, pl.ds(start, chunk)] = value

    def tile_second(c, start):
        return second[c, :, start + LANES:start + 2 * LANES]

    def put_second(c, start, value):
        second[c, :, start + LANES:start + 2 * LANES] = value

    def tile_out(c, start):
        return out_ref[c, :, start:start + LANES]

    def put_out(c, start, value):
        out_ref[c, :, start:start + LANES] = value

    build_faces()
    load_state.wait()
    split_up(first[:, :, inner].reshape(rows, width))
    face_out[0] = gather_face(first)
    pl.semaphore_wait(barrier, segs - 1 + has_before.astype(jnp.int32) + has_after.astype(jnp.int32))
    for copy in face_copies(0):
        copy.start()
    start_chain(first, 0)

    build_flips()
    along_k()
    load_metric.wait()
    inside_rates(first, finish_first)
    metric = jnp.where(on_first, geometry[3:6], geometry[6:9]).reshape(3 * length, width)
    split_up(metric)
    valid = jnp.where(jnp.logical_and(in_face, any_join), 1.0, 0.0)
    own_metric[...] = valid * gathered(metric[:, :LANES], metric[:, width - LANES:], 3 * length)
    own_face[...] = flipped(face_out[0])
    prepare_terms(step_one, flipped(own_metric[...]), own_face[...])

    await_chain(first, 0)
    chain_rates(first, 0, step_one, read_second, write_second)
    split_up(second[:, :, inner].reshape(rows, width))
    part_ref[...] = flipped(gather_face(second))
    for copy in face_copies(0):
        copy.wait_recv()
    added = face_rates(0, own_face[...])
    finished = part_ref[...] + added
    face_out[1] = finished
    for copy in face_copies(1):
        copy.start()

    spread(flipped(added), tile_second, put_second)
    start_chain(second, 1)
    own_face[...] = flipped(finished)
    split_up(second[:, :, inner].reshape(rows, width))
    along_k()
    inside_rates(second, finish_second)
    prepare_terms(step_two, own_metric[...], own_face[...])
    await_chain(second, 1)
    chain_rates(second, 1, step_two, read_out, write_out)
    for copy in face_copies(1):
        copy.wait_recv()
    spread(face_rates(1, own_face[...]), tile_out, put_out)

    for turn, padded in ((0, first), (1, second)):
        for copy in face_copies(turn):
            copy.wait_send()
        sent_chain(padded, turn)


def on_device(state, metric, block_map, links):
    segs, chain = lax.axis_size("seg"), lax.axis_size("blk")
    _, parts, length, width = state.shape
    cross = math.isqrt(width)
    assert cross <= HALF and length == 16
    chunk = math.lcm(cross, LANES)
    links = links.transpose(1, 2, 0)
    f32, bf16, dma = jnp.float32, jnp.bfloat16, pltpu.SemaphoreType.DMA
    result = pl.pallas_call(
        functools.partial(kernel, segs, chain, cross),
        out_shape=pltpu.VMEM((parts, length, width), f32),
        in_specs=[pl.BlockSpec(memory_space=pl.ANY)] * 4,
        out_specs=pl.BlockSpec(memory_space=pltpu.VMEM),
        scratch_shapes=[
            pltpu.VMEM((parts, length, width + 2 * LANES), f32),
            pltpu.VMEM((parts, length, width + 2 * LANES), f32),
            pltpu.VMEM((9, length, width), f32),
            pltpu.VMEM((width, LANES), bf16),
            pltpu.VMEM((2 * parts * length, width), bf16),
            pltpu.VMEM((2 * chunk, chunk), bf16),
            pltpu.VMEM((2 * chunk, chunk), bf16),
            pltpu.VMEM((2 * chunk, chunk), bf16),
            pltpu.VMEM((parts, length, width), f32),
            pltpu.VMEM((parts - 1, length, width), f32),
            pltpu.VMEM((parts * length, parts * length), bf16),
            pltpu.VMEM((2 * LANES, LANES), bf16),
            pltpu.VMEM((parts * length, LANES), f32),
            pltpu.VMEM(((parts - 1) * length, LANES), f32),
            pltpu.VMEM((5, length, LANES), f32),
            pltpu.VMEM((parts * length, LANES), f32),
            pltpu.VMEM((2, parts, 8, width), f32),
            pltpu.VMEM((2, parts * length, LANES), f32),
            pltpu.VMEM((2, segs - 1, parts * length, LANES), f32),
            pltpu.SMEM(block_map.shape, jnp.int32),
            pltpu.SMEM(links.shape, jnp.int32),
            dma((4,)), dma((2, 2)), dma((2, 2)), dma((2, segs - 1)), dma((2, segs - 1)),
        ],
        compiler_params=pltpu.CompilerParams(collective_id=0, has_side_effects=True),
    )(state, metric, block_map, links)
    return result.reshape(state.shape)


def solution(mesh):
    in_specs = (P(("seg", "blk"), None, None, None), P(("seg", "blk"), None, None, None), P(), P())
    out_specs = P(("seg", "blk"), None, None, None)
    return jax.shard_map(
        on_device, mesh=mesh, in_specs=in_specs, out_specs=out_specs, check_vma=False
    )
```

time: 16.6 us -> 13.2 us (0.80)
  Pallas kernels: 15.5 us -> 12.2 us
    pallas_call x1, Pallas kernels: 15.5 us -> 12.2 us  [on_device(): pl.pallas_call(functools.partial(kernel, segs, chain, cross), out_shape=p...]
where the time goes in v1:
time: 13.2 us; the launch traced here: 13.1 us
  Pallas kernels  12.2 us (92%)
  local copies, waits for them, and re-layouts  0.82 us (6%)
    pallas_call x1, Pallas kernels, on_device(): pl.pallas_call(functools.partial(kernel, segs, chain, cross), out_shape=p...  12.2 us
    unnamed x1, local copies, waits for them, and re-layouts  0.82 us

profile of v1, /device:TPU:1, one launch (start us, length us, event | category | flops | bytes accessed | tf_op | source)
XLA Modules:
  0.0 13.1 jit_solution(9208064137755459628)
XLA Ops:
  0.0 12.2 %shard_map.46 = f32[4,16,2304]{2,1,0:T(8,128)S(1)} custom-call(f32[1,4,16,2304]{3,2,1,0:T(8,128)} %state_hbm.1, f32[1,9,16,2304]{3,2,1,0:T(8,128)} %metric_hbm.1, s32[32]{0:T(128)} %block_map_hbm.1, s32[6,4,32]{2,1,0:T(4,128)} %bitcast.3), custom_call_target="tpu_custom_call" | custom-call | tf_op jit(solution)/shard_map/pallas_call | solution.py:531
  12.2 0.8 %copy.6 = f32[1,4,16,2304]{3,2,1,0:T(8,128)} copy(f32[1,4,16,2304]{3,2,1,0:T(8,128)S(1)} %bitcast.2) | data formatting | bytes 1179648

commit v2 on v1

--- a/solution.py
+++ b/solution.py
@@ -60,9 +60,10 @@
 
 
 def kernel(segs, chain, cross, state_hbm, metric_hbm, block_map_hbm, links_hbm, out_ref,
-           first, second, geometry, face_matrix, split, k_slope_uvw, k_slope_p, k_bend, slope_k, bend_k,
-           row_flip, lane_flip, own_face, own_metric, terms_ref, part_ref,
-           ghost_rows, face_out, face_in, block_map, links,
+           first, second, geometry, side_matrix, face_matrix, split, metric_split,
+           k_slope_uvw, k_slope_p, k_bend, slope_k, bend_k,
+           row_flip, lane_flip, terms_ref, added_ref, theirs_ref, turned_ref,
+           ghost_rows, end_rows, delta_out, delta_in, face_out, face_in, block_map, links,
            load_sem, chain_send, chain_recv, face_send, face_recv):
     length, width = out_ref.shape[1], out_ref.shape[2]
     rows = 4 * length
@@ -149,31 +150,49 @@
         padded[:, :, LANES + width:] = pads
     build_k()
 
+    def build_sides():
+        piece = 2 * LANES
+        cells = lax.broadcasted_iota(jnp.int32, (piece, LANES), 0)
+        place = jnp.where(in_face, face_place, 0)
+        for side, spot in enumerate((face_layer, cross - 1 - face_layer)):
+            source = jnp.where(in_face, place * cross + spot, -1)
+            for part in range(width // piece):
+                hit = (cells == source - part * piece).astype(jnp.float32).astype(jnp.bfloat16)
+                side_matrix[part * piece:(part + 1) * piece, side * LANES:(side + 1) * LANES] = hit
+
+    build_sides()
+
     load_map.wait()
     load_links.wait()
     block = block_map[me]
-    joins = [links[2 + side, 0, block] >= 0 for side in range(4)]
-    partner, flip_along, flip_across = jnp.int32(-1), jnp.int32(0), jnp.int32(0)
+
+    def joined_side(number):
+        return [links[2 + side, 0, number] >= 0 for side in range(4)]
+
+    joins = joined_side(block)
+    partner, partner_face = jnp.int32(-1), jnp.int32(0)
+    flip_along, flip_across = jnp.int32(0), jnp.int32(0)
     for side in range(4):
         partner = select(joins[side], links[2 + side, 0, block], partner)
+        partner_face = select(joins[side], links[2 + side, 1, block], partner_face)
         flip_along = select(joins[side], links[2 + side, 2, block], flip_along)
         flip_across = select(joins[side], links[2 + side, 3, block], flip_across)
     any_join = partner >= 0
     on_first = jnp.logical_or(joins[0], joins[1])
     on_second = jnp.logical_or(joins[2], joins[3])
     on_high = jnp.logical_or(joins[1], joins[3])
+    joins_before = joined_side(block_map[seg * chain + before])
+    joins_after = joined_side(block_map[seg * chain + after])
     comes_from = {offset: block_map[from_seg(offset) * chain + pos] == partner for offset in order}
     face_sign = select(on_high, -1.0, 1.0)
+    partner_sign = select(jnp.logical_or(partner_face == 3, partner_face == 5), -1.0, 1.0)
 
     def build_faces():
-        place = jnp.where(in_face, face_place, 0)
-        source = place * cross + select(on_high, cross - 1 - face_layer, face_layer)
-        source = jnp.where(jnp.logical_and(in_face, on_second), source, -1)
-        piece = 2 * LANES
-        cells = lax.broadcasted_iota(jnp.int32, (piece, LANES), 0)
-        for part in range(width // piece):
-            hit = cells == source - part * piece
-            face_matrix[part * piece:(part + 1) * piece, :] = hit.astype(jnp.float32).astype(jnp.bfloat16)
+        use_low = select(jnp.logical_and(on_second, jnp.logical_not(on_high)), 1.0, 0.0)
+        use_high = select(jnp.logical_and(on_second, on_high), 1.0, 0.0)
+        low = jnp.full((1, LANES), use_low).astype(jnp.bfloat16)
+        high = jnp.full((1, LANES), use_high).astype(jnp.bfloat16)
+        face_matrix[...] = side_matrix[:, :LANES] * low + side_matrix[:, LANES:] * high
 
     def build_flips():
         target = lax.broadcasted_iota(jnp.int32, (rows, 1), 0)
@@ -195,14 +214,14 @@
         both = jnp.dot(row_flip[:count, :count], both, preferred_element_type=jnp.float32)
         return jnp.dot(both.astype(jnp.bfloat16), lane_flip[...], preferred_element_type=jnp.float32)
 
-    def split_up(value):
+    def split_up(value, into):
         count = value.shape[0]
         lead, trail = halves(value)
-        split[:count] = lead
-        split[count:2 * count] = trail
-
-    def gathered(low, high, count):
-        packed = jnp.dot(split[:2 * count], face_matrix[...], preferred_element_type=jnp.float32)
+        into[:count] = lead
+        into[count:2 * count] = trail
+
+    def gathered(low, high, count, source):
+        packed = jnp.dot(source[...], face_matrix[...], preferred_element_type=jnp.float32)
         packed = packed[:count] + packed[count:]
         near, far = LANES - cross, LANES - 2 * cross
         lower = jnp.where(lane_row < HALF, low, pltpu.roll(low, HALF - cross, 1))
@@ -212,22 +231,25 @@
     def gather_face(padded):
         low = padded[:, :, LANES:2 * LANES].reshape(rows, LANES)
         high = padded[:, :, width:width + LANES].reshape(rows, LANES)
-        return gathered(low, high, rows)
-
-    def spread(value, read, write):
-        lead, trail = halves(value)
+        return gathered(low, high, rows, split)
+
+    near, far = LANES - cross, LANES - 2 * cross
+
+    def to_lower(value):
+        return jnp.where(lane_row < cross, value, pltpu.roll(value, LANES - (HALF - cross), 1))
+
+    def to_upper(value):
+        return jnp.where(lane_row >= near, pltpu.roll(value, near, 1), pltpu.roll(value, LANES - (HALF - far), 1))
+
+    def spread(value, both, matrix, lower, upper, write):
+        count = value.shape[0]
+        lead, trail = halves(both)
         both = jnp.concatenate([lead, trail], axis=0)
-        near, far = LANES - cross, LANES - 2 * cross
-        lower = jnp.where(lane_row < cross, value, pltpu.roll(value, LANES - (HALF - cross), 1))
-        lower = jnp.where(jnp.logical_and(lane_row < 2 * cross, jnp.logical_and(on_first, jnp.logical_not(on_high))),
-                          lower, 0.0)
-        upper = jnp.where(lane_row >= near, pltpu.roll(value, near, 1), pltpu.roll(value, LANES - (HALF - far), 1))
-        upper = jnp.where(jnp.logical_and(lane_row >= far, jnp.logical_and(on_first, on_high)), upper, 0.0)
         piece = 2 * LANES
         for part in range(width // piece):
-            out = lax.dot_general(both, face_matrix[part * piece:(part + 1) * piece, :],
+            out = lax.dot_general(both, matrix[part * piece:(part + 1) * piece, :],
                                   (((1,), (1,)), ((), ())), preferred_element_type=jnp.float32)
-            out = out[:rows] + out[rows:]
+            out = out[:count] + out[count:]
             for tile in range(2):
                 start = part * piece + tile * LANES
                 add = out[:, tile * LANES:(tile + 1) * LANES]
@@ -235,8 +257,39 @@
                     add = add + lower
                 if start == width - LANES:
                     add = add + upper
-                for c in range(4):
-                    write(c, start, read(c, start) + add[c * length:(c + 1) * length])
+                write(start, add)
+
+    def spread_face(value, read, write):
+        on_low = jnp.logical_not(on_high)
+        lower = jnp.where(jnp.logical_and(lane_row < 2 * cross, jnp.logical_and(on_first, on_low)), to_lower(value), 0.0)
+        upper = jnp.where(jnp.logical_and(lane_row >= far, jnp.logical_and(on_first, on_high)), to_upper(value), 0.0)
+
+        def put(start, add):
+            for c in range(4):
+                write(c, start, read(c, start) + add[c * length:(c + 1) * length])
+
+        spread(value, value, face_matrix, lower, upper, put)
+
+    def spread_delta():
+        end_row = lax.broadcasted_iota(jnp.int32, (8, LANES), 0)
+        wanted = jnp.logical_or(jnp.logical_and(end_row < 2, has_before), jnp.logical_and(end_row >= 6, has_after))
+        value = jnp.concatenate([jnp.where(wanted, delta_in[c], 0.0) for c in range(4)], axis=0)
+
+        def mask(side):
+            flag = [select(flags[side], 1.0, 0.0) for flags in (joins_before, joins_after)]
+            one = jnp.where(end_row < 4, flag[0], flag[1])
+            return jnp.concatenate([one] * 4, axis=0)
+
+        lower = jnp.where(lane_row < 2 * cross, to_lower(value) * mask(0), 0.0)
+        upper = jnp.where(lane_row >= far, to_upper(value) * mask(1), 0.0)
+        both = jnp.concatenate([value * mask(2), value * mask(3)], axis=1)
+
+        def put(start, add):
+            for c in range(4):
+                at = slice(start, start + LANES)
+                ghost_rows[1, c, :, at] = ghost_rows[1, c, :, at] + add[c * 8:(c + 1) * 8]
+
+        spread(value, both, side_matrix, lower, upper, put)
 
     def along_k():
         count = 3 * length
@@ -255,23 +308,38 @@
             bend_k[:, :, at] = bend[step * count:(step + 1) * count].reshape(3, length, chunk)
             slope_k[3, :, at] = slope_p[step * length:(step + 1) * length]
 
-    def chain_copies(padded, turn):
+    def chain_copies(kind):
+        if kind == 0:
+            low, high = first.at[:, 0:2, inner], first.at[:, length - 2:length, inner]
+        else:
+            source = end_rows if kind == 1 else delta_out
+            low, high = source.at[:, 0:2], source.at[:, 6:8]
+        target = delta_in if kind == 2 else ghost_rows.at[kind]
         to_before = pltpu.make_async_remote_copy(
-            padded.at[:, 0:2, inner], ghost_rows.at[turn, :, 6:8], chain_send.at[turn, 0], chain_recv.at[turn, 0],
+            low, target.at[:, 6:8], chain_send.at[kind, 0], chain_recv.at[kind, 0],
             device_id={"blk": before}, device_id_type=MESH)
         to_after = pltpu.make_async_remote_copy(
-            padded.at[:, length - 2:length, inner], ghost_rows.at[turn, :, 0:2],
-            chain_send.at[turn, 1], chain_recv.at[turn, 1], device_id={"blk": after}, device_id_type=MESH)
+            high, target.at[:, 0:2], chain_send.at[kind, 1], chain_recv.at[kind, 1],
+            device_id={"blk": after}, device_id_type=MESH)
         return to_before, to_after
 
-    def face_copies(turn):
+    def face_copies(kind):
+        used = pl.ds(0, 3 * length if kind == 1 else rows)
         return [pltpu.make_async_remote_copy(
-            face_out.at[turn], face_in.at[turn, offset - 1], face_send.at[turn, offset - 1],
-            face_recv.at[turn, offset - 1], device_id={"seg": to_seg(offset)}, device_id_type=MESH)
+            face_out.at[kind, used], face_in.at[kind, offset - 1, used], face_send.at[kind, offset - 1],
+            face_recv.at[kind, offset - 1], device_id={"seg": to_seg(offset)}, device_id_type=MESH)
             for offset in order]
 
-    def start_chain(padded, turn):
-        to_before, to_after = chain_copies(padded, turn)
+    def start_faces(kind):
+        for copy in face_copies(kind):
+            copy.start()
+
+    def await_faces(kind):
+        for copy in face_copies(kind):
+            copy.wait_recv()
+
+    def start_chain(kind):
+        to_before, to_after = chain_copies(kind)
 
         @pl.when(has_before)
         def _():
@@ -281,6 +349,7 @@
         def _():
             to_after.start()
 
+    def open_ends(padded, turn):
         @pl.when(jnp.logical_not(has_before))
         def _():
             for c in range(4):
@@ -293,8 +362,8 @@
                 ghost_rows[turn, c, 6:7, :] = -WALL[c] * padded[c, length - 1:length, inner]
                 ghost_rows[turn, c, 7:8, :] = -WALL[c] * padded[c, length - 2:length - 1, inner]
 
-    def await_chain(padded, turn):
-        to_before, to_after = chain_copies(padded, turn)
+    def await_chain(kind):
+        to_before, to_after = chain_copies(kind)
 
         @pl.when(has_before)
         def _():
@@ -304,8 +373,8 @@
         def _():
             to_before.wait_recv()
 
-    def sent_chain(padded, turn):
-        to_before, to_after = chain_copies(padded, turn)
+    def sent_chain(kind):
+        to_before, to_after = chain_copies(kind)
 
         @pl.when(has_before)
         def _():
@@ -391,7 +460,7 @@
     near_row = jnp.where(jnp.logical_or(sub == 0, sub == 7), 1.0, 0.0)
     row_sign = jnp.where(sub < 4, 1.0, -1.0)
 
-    def chain_rates(padded, turn, scale, read, write):
+    def chain_rates(padded, turn, scale, read, write, keep=None):
         def body(step, carry):
             start = pl.multiple_of(step * chunk, LANES)
             at = pl.ds(start, chunk)
@@ -405,10 +474,14 @@
             moved = [ghost_rows[turn, c, :, at] for c in range(4)]
             ghosts = [ends(pltpu.roll(m, 7, 0), pltpu.roll(m, 1, 0)) for m in moved]
             sums = ghost_rates(near_row, ghost_terms(scale, row_sign, near_row, metric, values), ghosts, moved)
+            low, high = pl.ds(0, 8), pl.ds(length - 8, 8)
             for c in range(4):
-                write(c, pl.ds(0, 8), start, read(c, pl.ds(0, 8), start) + jnp.where(sub < 2, sums[c], 0.0))
-                high = pl.ds(length - 8, 8)
-                write(c, high, start, read(c, high, start) + jnp.where(sub >= 6, sums[c], 0.0))
+                low_new = read(c, low, start) + jnp.where(sub < 2, sums[c], 0.0)
+                high_new = read(c, high, start) + jnp.where(sub >= 6, sums[c], 0.0)
+                write(c, low, start, low_new)
+                write(c, high, start, high_new)
+                if keep is not None:
+                    keep[c, :, at] = ends(low_new, high_new)
             return carry
 
         lax.fori_loop(0, chunks, body, 0)
@@ -416,21 +489,29 @@
     def at_part(value, c):
         return value[c * length:(c + 1) * length]
 
+    def terms_of(scale, sign, metric, own):
+        return ghost_terms(scale, sign, near_lane, [at_part(metric, b) for b in range(3)],
+                           [at_part(own, b) for b in range(3)])
+
     def prepare_terms(scale, metric, own):
-        edge, outer, pull = ghost_terms(scale, face_sign, near_lane, [at_part(metric, b) for b in range(3)],
-                                        [at_part(own, b) for b in range(3)])
+        edge, outer, pull = terms_of(scale, face_sign, metric, own)
         terms_ref[0] = edge
         terms_ref[1] = outer
         for b in range(3):
             terms_ref[2 + b] = pull[b]
 
-    def face_rates(turn, own):
-        received = face_in[turn, order[-1] - 1]
+    def own_terms():
+        return terms_ref[0], terms_ref[1], [terms_ref[2 + b] for b in range(3)]
+
+    def received(kind, count):
+        value = face_in[kind, order[-1] - 1, :count]
         for offset in order[:-1]:
-            received = jnp.where(comes_from[offset], face_in[turn, offset - 1], received)
-        ghosts = [at_part(received, c) - WALL[c] * at_part(own, c) for c in range(4)]
+            value = jnp.where(comes_from[offset], face_in[kind, offset - 1, :count], value)
+        return value
+
+    def face_rates(terms, theirs, own):
+        ghosts = [at_part(theirs, c) - WALL[c] * at_part(own, c) for c in range(4)]
         moved = [pltpu.roll(g, HALF, 1) for g in ghosts]
-        terms = (terms_ref[0], terms_ref[1], [terms_ref[2 + b] for b in range(3)])
         return jnp.concatenate(ghost_rates(near_lane, terms, ghosts, moved), axis=0)
 
     def inside_second(start, size):
@@ -471,53 +552,63 @@
 
     build_faces()
     load_state.wait()
-    split_up(first[:, :, inner].reshape(rows, width))
+    split_up(first[:, :, inner].reshape(rows, width), split)
     face_out[0] = gather_face(first)
     pl.semaphore_wait(barrier, segs - 1 + has_before.astype(jnp.int32) + has_after.astype(jnp.int32))
-    for copy in face_copies(0):
-        copy.start()
-    start_chain(first, 0)
-
+    start_faces(0)
+    start_chain(0)
+
+    load_metric.wait()
+    metric = jnp.where(on_first, geometry[3:6], geometry[6:9]).reshape(3 * length, width)
+    split_up(metric, metric_split)
+    valid = jnp.where(jnp.logical_and(in_face, any_join), 1.0, 0.0)
+    own_metric = valid * gathered(metric[:, :LANES], metric[:, width - LANES:], 3 * length, metric_split)
+    face_out[1, :3 * length] = own_metric
+    start_faces(1)
+    open_ends(first, 0)
     build_flips()
+    prepare_terms(step_one, own_metric, face_out[0])
     along_k()
-    load_metric.wait()
     inside_rates(first, finish_first)
-    metric = jnp.where(on_first, geometry[3:6], geometry[6:9]).reshape(3 * length, width)
-    split_up(metric)
-    valid = jnp.where(jnp.logical_and(in_face, any_join), 1.0, 0.0)
-    own_metric[...] = valid * gathered(metric[:, :LANES], metric[:, width - LANES:], 3 * length)
-    own_face[...] = flipped(face_out[0])
-    prepare_terms(step_one, flipped(own_metric[...]), own_face[...])
-
-    await_chain(first, 0)
-    chain_rates(first, 0, step_one, read_second, write_second)
-    split_up(second[:, :, inner].reshape(rows, width))
-    part_ref[...] = flipped(gather_face(second))
-    for copy in face_copies(0):
-        copy.wait_recv()
-    added = face_rates(0, own_face[...])
-    finished = part_ref[...] + added
-    face_out[1] = finished
-    for copy in face_copies(1):
-        copy.start()
-
-    spread(flipped(added), tile_second, put_second)
-    start_chain(second, 1)
-    own_face[...] = flipped(finished)
-    split_up(second[:, :, inner].reshape(rows, width))
+
+    await_chain(0)
+    chain_rates(first, 0, step_one, read_second, write_second, end_rows)
+    start_chain(1)
+    split_up(second[:, :, inner].reshape(rows, width), split)
+    face_out[2] = gather_face(second)
+    start_faces(2)
+
+    turned_ref[...] = flipped(face_out[0])
+    await_faces(0)
+    added = face_rates(own_terms(), flipped(received(0, rows)), face_out[0])
+    for c in range(4):
+        delta_out[c] = jnp.where(lax.broadcasted_iota(jnp.int32, (8, LANES), 0) < 4,
+                                 added[c * length:c * length + 8], added[(c + 1) * length - 8:(c + 1) * length])
+    start_chain(2)
+    added_ref[...] = face_out[2] + added
+    spread_face(added, tile_second, put_second)
+    open_ends(second, 1)
+    split_up(second[:, :, inner].reshape(rows, width), split)
     along_k()
     inside_rates(second, finish_second)
-    prepare_terms(step_two, own_metric[...], own_face[...])
-    await_chain(second, 1)
+    prepare_terms(step_two, face_out[1, :3 * length], added_ref[...])
+    await_faces(1)
+    their_face = received(0, rows)
+    their_terms = terms_of(step_one, partner_sign, received(1, 3 * length), their_face)
+    theirs_ref[...] = face_rates(their_terms, turned_ref[...], their_face)
+
+    await_chain(1)
+    await_chain(2)
+    spread_delta()
     chain_rates(second, 1, step_two, read_out, write_out)
-    for copy in face_copies(1):
-        copy.wait_recv()
-    spread(face_rates(1, own_face[...]), tile_out, put_out)
-
-    for turn, padded in ((0, first), (1, second)):
-        for copy in face_copies(turn):
+    await_faces(2)
+    their_face = flipped(received(2, rows) + theirs_ref[...])
+    spread_face(face_rates(own_terms(), their_face, added_ref[...]), tile_out, put_out)
+
+    for kind in range(3):
+        for copy in face_copies(kind):
             copy.wait_send()
-        sent_chain(padded, turn)
+        sent_chain(kind)
 
 
 def on_device(state, metric, block_map, links):
@@ -537,8 +628,10 @@
             pltpu.VMEM((parts, length, width + 2 * LANES), f32),
             pltpu.VMEM((parts, length, width + 2 * LANES), f32),
             pltpu.VMEM((9, length, width), f32),
+            pltpu.VMEM((width, 2 * LANES), bf16),
             pltpu.VMEM((width, LANES), bf16),
             pltpu.VMEM((2 * parts * length, width), bf16),
+            pltpu.VMEM((2 * (parts - 1) * length, width), bf16),
             pltpu.VMEM((2 * chunk, chunk), bf16),
             pltpu.VMEM((2 * chunk, chunk), bf16),
             pltpu.VMEM((2 * chunk, chunk), bf16),
@@ -546,16 +639,19 @@
             pltpu.VMEM((parts - 1, length, width), f32),
             pltpu.VMEM((parts * length, parts * length), bf16),
             pltpu.VMEM((2 * LANES, LANES), bf16),
-            pltpu.VMEM((parts * length, LANES), f32),
-            pltpu.VMEM(((parts - 1) * length, LANES), f32),
             pltpu.VMEM((5, length, LANES), f32),
             pltpu.VMEM((parts * length, LANES), f32),
+            pltpu.VMEM((parts * length, LANES), f32),
+            pltpu.VMEM((parts * length, LANES), f32),
             pltpu.VMEM((2, parts, 8, width), f32),
-            pltpu.VMEM((2, parts * length, LANES), f32),
-            pltpu.VMEM((2, segs - 1, parts * length, LANES), f32),
+            pltpu.VMEM((parts, 8, width), f32),
+            pltpu.VMEM((parts, 8, LANES), f32),
+            pltpu.VMEM((parts, 8, LANES), f32),
+            pltpu.VMEM((3, parts * length, LANES), f32),
+            pltpu.VMEM((3, segs - 1, parts * length, LANES), f32),
             pltpu.SMEM(block_map.shape, jnp.int32),
             pltpu.SMEM(links.shape, jnp.int32),
-            dma((4,)), dma((2, 2)), dma((2, 2)), dma((2, segs - 1)), dma((2, segs - 1)),
+            dma((4,)), dma((3, 2)), dma((3, 2)), dma((3, segs - 1)), dma((3, segs - 1)),
         ],
         compiler_params=pltpu.CompilerParams(collective_id=0, has_side_effects=True),
     )(state, metric, block_map, links)

time: 13.2 us -> 13.9 us (1.053)
  Pallas kernels: 12.2 us -> 13 us
    pallas_call x1, Pallas kernels: 12.2 us -> 13 us  [on_device(): pl.pallas_call(functools.partial(kernel, segs, chain, cross), out_shape=p...]
where the time goes in v2:
time: 13.9 us; the launch traced here: 13.8 us
  Pallas kernels  13 us (94%)
  local copies, waits for them, and re-layouts  0.82 us (6%)
    pallas_call x1, Pallas kernels, on_device(): pl.pallas_call(functools.partial(kernel, segs, chain, cross), out_shape=p...  13 us
    unnamed x1, local copies, waits for them, and re-layouts  0.82 us

profile of v2, /device:TPU:1, one launch (start us, length us, event | category | flops | bytes accessed | tf_op | source)
XLA Modules:
  0.0 13.8 jit_solution(784653381773006044)
XLA Ops:
  0.0 13.0 %shard_map.46 = f32[4,16,2304]{2,1,0:T(8,128)S(1)} custom-call(f32[1,4,16,2304]{3,2,1,0:T(8,128)} %state_hbm.1, f32[1,9,16,2304]{3,2,1,0:T(8,128)} %metric_hbm.1, s32[32]{0:T(128)} %block_map_hbm.1, s32[6,4,32]{2,1,0:T(4,128)} %bitcast.3), custom_call_target="tpu_custom_call" | custom-call | tf_op jit(solution)/shard_map/pallas_call | solution.py:622
  13.0 0.8 %copy.6 = f32[1,4,16,2304]{3,2,1,0:T(8,128)} copy(f32[1,4,16,2304]{3,2,1,0:T(8,128)S(1)} %bitcast.2) | data formatting | bytes 1179648

commit v3 on v2

--- a/solution.py
+++ b/solution.py
@@ -24,6 +24,14 @@
     return quotient, index - size * quotient
 
 
+def take(value, index, axis):
+    numbers = lax.GatherDimensionNumbers(
+        offset_dims=(), collapsed_slice_dims=(axis,), start_index_map=(axis,),
+        operand_batching_dims=(1 - axis,), start_indices_batching_dims=(1 - axis,))
+    return lax.gather(value, index[..., None], numbers, slice_sizes=(1, 1),
+                      mode=lax.GatherScatterMode.PROMISE_IN_BOUNDS)
+
+
 def flipped_bits(index, bits):
     bit = 1
     while bit <= bits:
@@ -60,9 +68,9 @@
 
 
 def kernel(segs, chain, cross, state_hbm, metric_hbm, block_map_hbm, links_hbm, out_ref,
-           first, second, geometry, side_matrix, face_matrix, split, metric_split,
+           first, second, geometry, face_index, face_mask, delta_index, delta_mask, split,
            k_slope_uvw, k_slope_p, k_bend, slope_k, bend_k,
-           row_flip, lane_flip, terms_ref, added_ref, theirs_ref, turned_ref,
+           terms_ref, added_ref, theirs_ref, turned_ref,
            ghost_rows, end_rows, delta_out, delta_in, face_out, face_in, block_map, links,
            load_sem, chain_send, chain_recv, face_send, face_recv):
     length, width = out_ref.shape[1], out_ref.shape[2]
@@ -149,18 +157,6 @@
         padded[:, :, :LANES] = pads
         padded[:, :, LANES + width:] = pads
     build_k()
-
-    def build_sides():
-        piece = 2 * LANES
-        cells = lax.broadcasted_iota(jnp.int32, (piece, LANES), 0)
-        place = jnp.where(in_face, face_place, 0)
-        for side, spot in enumerate((face_layer, cross - 1 - face_layer)):
-            source = jnp.where(in_face, place * cross + spot, -1)
-            for part in range(width // piece):
-                hit = (cells == source - part * piece).astype(jnp.float32).astype(jnp.bfloat16)
-                side_matrix[part * piece:(part + 1) * piece, side * LANES:(side + 1) * LANES] = hit
-
-    build_sides()
 
     load_map.wait()
     load_links.wait()
@@ -187,32 +183,57 @@
     face_sign = select(on_high, -1.0, 1.0)
     partner_sign = select(jnp.logical_or(partner_face == 3, partner_face == 5), -1.0, 1.0)
 
+    lane_of = lax.broadcasted_iota(jnp.int32, (8, LANES), 1)
+    row_in = lax.broadcasted_iota(jnp.int32, (8, LANES), 0)
+    layer_of = (lane_of >= HALF).astype(jnp.int32)
+    place_of = lane_of - HALF * layer_of
+    face_lane = place_of < cross
+
+    def spread_index(tile, high):
+        start = tile * LANES
+        row = start // cross
+        spot = lane_of + (start - row * cross)
+        place = jnp.full((8, LANES), row, jnp.int32)
+        for step in range(1, LANES // cross + 2):
+            past = spot >= step * cross
+            place = place + past.astype(jnp.int32)
+        spot = lane_of + start - place * cross
+        layer = jnp.where(high, cross - 1 - spot, spot)
+        return jnp.where(layer < 2, place + HALF * layer, -1)
+
+    def build_spread(index_ref, mask_ref, high, used):
+        for tile in range(width // LANES):
+            index = jnp.where(used, spread_index(tile, high), -1)
+            mask_ref[tile] = jnp.where(index >= 0, 1.0, 0.0)
+            index_ref[tile] = jnp.maximum(index, 0)
+
     def build_faces():
-        use_low = select(jnp.logical_and(on_second, jnp.logical_not(on_high)), 1.0, 0.0)
-        use_high = select(jnp.logical_and(on_second, on_high), 1.0, 0.0)
-        low = jnp.full((1, LANES), use_low).astype(jnp.bfloat16)
-        high = jnp.full((1, LANES), use_high).astype(jnp.bfloat16)
-        face_matrix[...] = side_matrix[:, :LANES] * low + side_matrix[:, LANES:] * high
-
-    def build_flips():
-        target = lax.broadcasted_iota(jnp.int32, (rows, 1), 0)
-        component, along_index = split_index(target, length, 4)
-        along_index = select(flip_along == 1, length - 1 - along_index, along_index)
-        target = component * length + along_index
-        hit = lax.broadcasted_iota(jnp.int32, (rows, rows), 1) == target
-        row_flip[...] = hit.astype(jnp.float32).astype(jnp.bfloat16)
-        place = select(flip_across == 1, cross - 1 - face_place, face_place)
-        origin = jnp.where(in_face, face_layer * HALF + place, -1)
-        hit = lax.broadcasted_iota(jnp.int32, (LANES, LANES), 0) == origin
-        hit = hit.astype(jnp.float32).astype(jnp.bfloat16)
-        lane_flip[:LANES, :] = hit
-        lane_flip[LANES:, :] = hit
+        build_spread(face_index, face_mask, jnp.full((8, LANES), select(on_high, 1, 0)) > 0,
+                     jnp.full((8, LANES), select(on_second, 1, 0)) > 0)
+
+    def build_delta():
+        def chosen(sides):
+            flags = [select(jnp.logical_or(near_joins[sides[0]], near_joins[sides[1]]), 1, 0)
+                     for near_joins in (joins_before, joins_after)]
+            return jnp.where(row_in < 4, flags[0], flags[1]) > 0
+
+        build_spread(delta_index, delta_mask, chosen((1, 3)), chosen((2, 3)))
+
+    source_of = jnp.where(face_lane, place_of, 0) * cross + select(on_high, cross - 1 - layer_of, layer_of)
+    source_tile, source_lane = split_index(source_of, LANES, width // LANES)
+    flip_rows = select(flip_along == 1, 7 - row_in, row_in)
+    flip_lanes = jnp.where(face_lane, layer_of * HALF + select(flip_across == 1, cross - 1 - place_of, place_of), lane_of)
+
+    def by_rows(value, function):
+        return jnp.concatenate([function(value[at:at + 8]) for at in range(0, value.shape[0], 8)], axis=0)
 
     def flipped(value):
-        count = value.shape[0]
-        both = jnp.concatenate(halves(value), axis=1)
-        both = jnp.dot(row_flip[:count, :count], both, preferred_element_type=jnp.float32)
-        return jnp.dot(both.astype(jnp.bfloat16), lane_flip[...], preferred_element_type=jnp.float32)
+        parts = []
+        for at in range(0, value.shape[0], length):
+            low, high = value[at:at + 8], value[at + 8:at + 16]
+            for half in (select(flip_along == 1, high, low), select(flip_along == 1, low, high)):
+                parts.append(take(take(half, flip_rows, 0), flip_lanes, 1))
+        return jnp.concatenate(parts, axis=0)
 
     def split_up(value, into):
         count = value.shape[0]
@@ -220,18 +241,29 @@
         into[:count] = lead
         into[count:2 * count] = trail
 
-    def gathered(low, high, count, source):
-        packed = jnp.dot(source[...], face_matrix[...], preferred_element_type=jnp.float32)
-        packed = packed[:count] + packed[count:]
+    def gathered(low, high, tile_of):
+        packed = None
+        for tile in range(width // LANES):
+            part = by_rows(tile_of(tile), lambda x: take(x, source_lane, 1))
+            here = jnp.concatenate([source_tile == tile] * (part.shape[0] // 8), axis=0)
+            packed = part if packed is None else jnp.where(here, part, packed)
         near, far = LANES - cross, LANES - 2 * cross
         lower = jnp.where(lane_row < HALF, low, pltpu.roll(low, HALF - cross, 1))
         upper = jnp.where(lane_row < HALF, pltpu.roll(high, LANES - near, 1), pltpu.roll(high, HALF - far, 1))
         return jnp.where(on_first, jnp.where(on_high, upper, lower), packed)
 
     def gather_face(padded):
-        low = padded[:, :, LANES:2 * LANES].reshape(rows, LANES)
-        high = padded[:, :, width:width + LANES].reshape(rows, LANES)
-        return gathered(low, high, rows, split)
+        def tile_of(tile):
+            start = LANES + tile * LANES
+            return padded[:, :, start:start + LANES].reshape(rows, LANES)
+
+        return gathered(tile_of(0), tile_of(width // LANES - 1), tile_of)
+
+    def gather_metric():
+        def tile_of(tile, base=6):
+            return geometry[base:base + 3, :, tile * LANES:(tile + 1) * LANES].reshape(3 * length, LANES)
+
+        return gathered(tile_of(0, 3), tile_of(width // LANES - 1, 3), tile_of)
 
     near, far = LANES - cross, LANES - 2 * cross
 
@@ -241,23 +273,15 @@
     def to_upper(value):
         return jnp.where(lane_row >= near, pltpu.roll(value, near, 1), pltpu.roll(value, LANES - (HALF - far), 1))
 
-    def spread(value, both, matrix, lower, upper, write):
-        count = value.shape[0]
-        lead, trail = halves(both)
-        both = jnp.concatenate([lead, trail], axis=0)
-        piece = 2 * LANES
-        for part in range(width // piece):
-            out = lax.dot_general(both, matrix[part * piece:(part + 1) * piece, :],
-                                  (((1,), (1,)), ((), ())), preferred_element_type=jnp.float32)
-            out = out[:count] + out[count:]
-            for tile in range(2):
-                start = part * piece + tile * LANES
-                add = out[:, tile * LANES:(tile + 1) * LANES]
-                if start == 0:
-                    add = add + lower
-                if start == width - LANES:
-                    add = add + upper
-                write(start, add)
+    def spread(value, index_ref, mask_ref, lower, upper, write):
+        for tile in range(width // LANES):
+            index, mask = index_ref[tile], mask_ref[tile]
+            add = by_rows(value, lambda x: take(x, index, 1) * mask)
+            if tile == 0:
+                add = add + lower
+            if tile == width // LANES - 1:
+                add = add + upper
+            write(tile * LANES, add)
 
     def spread_face(value, read, write):
         on_low = jnp.logical_not(on_high)
@@ -268,7 +292,7 @@
             for c in range(4):
                 write(c, start, read(c, start) + add[c * length:(c + 1) * length])
 
-        spread(value, value, face_matrix, lower, upper, put)
+        spread(value, face_index, face_mask, lower, upper, put)
 
     def spread_delta():
         end_row = lax.broadcasted_iota(jnp.int32, (8, LANES), 0)
@@ -282,14 +306,12 @@
 
         lower = jnp.where(lane_row < 2 * cross, to_lower(value) * mask(0), 0.0)
         upper = jnp.where(lane_row >= far, to_upper(value) * mask(1), 0.0)
-        both = jnp.concatenate([value * mask(2), value * mask(3)], axis=1)
-
         def put(start, add):
             for c in range(4):
                 at = slice(start, start + LANES)
                 ghost_rows[1, c, :, at] = ghost_rows[1, c, :, at] + add[c * 8:(c + 1) * 8]
 
-        spread(value, both, side_matrix, lower, upper, put)
+        spread(value, delta_index, delta_mask, lower, upper, put)
 
     def along_k():
         count = 3 * length
@@ -550,31 +572,28 @@
     def put_out(c, start, value):
         out_ref[c, :, start:start + LANES] = value
 
-    build_faces()
     load_state.wait()
-    split_up(first[:, :, inner].reshape(rows, width), split)
     face_out[0] = gather_face(first)
     pl.semaphore_wait(barrier, segs - 1 + has_before.astype(jnp.int32) + has_after.astype(jnp.int32))
     start_faces(0)
     start_chain(0)
 
     load_metric.wait()
-    metric = jnp.where(on_first, geometry[3:6], geometry[6:9]).reshape(3 * length, width)
-    split_up(metric, metric_split)
     valid = jnp.where(jnp.logical_and(in_face, any_join), 1.0, 0.0)
-    own_metric = valid * gathered(metric[:, :LANES], metric[:, width - LANES:], 3 * length, metric_split)
+    own_metric = valid * gather_metric()
     face_out[1, :3 * length] = own_metric
     start_faces(1)
     open_ends(first, 0)
-    build_flips()
+    build_faces()
+    build_delta()
     prepare_terms(step_one, own_metric, face_out[0])
+    split_up(first[:, :, inner].reshape(rows, width), split)
     along_k()
     inside_rates(first, finish_first)
 
     await_chain(0)
     chain_rates(first, 0, step_one, read_second, write_second, end_rows)
     start_chain(1)
-    split_up(second[:, :, inner].reshape(rows, width), split)
     face_out[2] = gather_face(second)
     start_faces(2)
 
@@ -628,17 +647,16 @@
             pltpu.VMEM((parts, length, width + 2 * LANES), f32),
             pltpu.VMEM((parts, length, width + 2 * LANES), f32),
             pltpu.VMEM((9, length, width), f32),
-            pltpu.VMEM((width, 2 * LANES), bf16),
-            pltpu.VMEM((width, LANES), bf16),
+            pltpu.VMEM((width // LANES, 8, LANES), jnp.int32),
+            pltpu.VMEM((width // LANES, 8, LANES), f32),
+            pltpu.VMEM((width // LANES, 8, LANES), jnp.int32),
+            pltpu.VMEM((width // LANES, 8, LANES), f32),
             pltpu.VMEM((2 * parts * length, width), bf16),
-            pltpu.VMEM((2 * (parts - 1) * length, width), bf16),
             pltpu.VMEM((2 * chunk, chunk), bf16),
             pltpu.VMEM((2 * chunk, chunk), bf16),
             pltpu.VMEM((2 * chunk, chunk), bf16),
             pltpu.VMEM((parts, length, width), f32),
             pltpu.VMEM((parts - 1, length, width), f32),
-            pltpu.VMEM((parts * length, parts * length), bf16),
-            pltpu.VMEM((2 * LANES, LANES), bf16),
             pltpu.VMEM((5, length, LANES), f32),
             pltpu.VMEM((parts * length, LANES), f32),
             pltpu.VMEM((parts * length, LANES), f32),

time: 13.9 us -> 13 us (0.935)
  Pallas kernels: 13 us -> 12 us
    pallas_call x1, Pallas kernels: 13 us -> 12 us  [on_device(): pl.pallas_call(functools.partial(kernel, segs, chain, cross), out_shape=p...]
where the time goes in v3:
time: 13 us; the launch traced here: 12.8 us
  Pallas kernels  12 us (92%)
  local copies, waits for them, and re-layouts  0.82 us (6%)
    pallas_call x1, Pallas kernels, on_device(): pl.pallas_call(functools.partial(kernel, segs, chain, cross), out_shape=p...  12 us
    unnamed x1, local copies, waits for them, and re-layouts  0.82 us

profile of v3, /device:TPU:1, one launch (start us, length us, event | category | flops | bytes accessed | tf_op | source)
XLA Modules:
  0.0 12.8 jit_solution(9090779518438024686)
XLA Ops:
  0.0 12.0 %shard_map.46 = f32[4,16,2304]{2,1,0:T(8,128)S(1)} custom-call(f32[1,4,16,2304]{3,2,1,0:T(8,128)} %state_hbm.1, f32[1,9,16,2304]{3,2,1,0:T(8,128)} %metric_hbm.1, s32[32]{0:T(128)} %block_map_hbm.1, s32[6,4,32]{2,1,0:T(4,128)} %bitcast.3), custom_call_target="tpu_custom_call" | custom-call | tf_op jit(solution)/shard_map/pallas_call | solution.py:641
  12.0 0.8 %copy.6 = f32[1,4,16,2304]{3,2,1,0:T(8,128)} copy(f32[1,4,16,2304]{3,2,1,0:T(8,128)S(1)} %bitcast.2) | data formatting | bytes 1179648

commit v4 on v3

--- a/solution.py
+++ b/solution.py
@@ -69,7 +69,7 @@
 
 def kernel(segs, chain, cross, state_hbm, metric_hbm, block_map_hbm, links_hbm, out_ref,
            first, second, geometry, face_index, face_mask, delta_index, delta_mask, split,
-           k_slope_uvw, k_slope_p, k_bend, slope_k, bend_k,
+           k_slope_uvw, k_slope_p, k_bend, i_matrix, slope_k, bend_k, slope_i, bend_i, norms,
            terms_ref, added_ref, theirs_ref, turned_ref,
            ghost_rows, end_rows, delta_out, delta_in, face_out, face_in, block_map, links,
            load_sem, chain_send, chain_recv, face_send, face_recv):
@@ -138,8 +138,7 @@
                     return jnp.where(index == value, factor, 0.0)
 
                 slope = at(offset, -2, 1.0) + at(offset, -1, -8.0) + at(offset, 1, 8.0) + at(offset, 2, -1.0)
-                bend = (at(offset, -2, -1.0) + at(offset, -1, 16.0) + at(offset, 0, -30.0)
-                        + at(offset, 1, 16.0) + at(offset, 2, -1.0))
+                bend = at(offset, -2, -1.0) + at(offset, -1, 16.0) + at(offset, 1, 16.0) + at(offset, 2, -1.0)
                 end = 2 * cross - 2
                 wall_slope = (at(mirrored, 0, -8.0) + at(mirrored, 1, 1.0)
                               + at(mirrored, end, 8.0) + at(mirrored, end - 1, -1.0))
@@ -157,6 +156,23 @@
         padded[:, :, :LANES] = pads
         padded[:, :, LANES + width:] = pads
     build_k()
+
+    def build_i():
+        count = 7 * length
+        term, here = split_index(lax.broadcasted_iota(jnp.int32, (count, LANES), 0), length, 7)
+        part, there = split_index(lax.broadcasted_iota(jnp.int32, (count, LANES), 1), length, 8)
+        part = jnp.where(part >= 4, part - 4, part)
+        offset = there - here
+
+        def at(index, factor):
+            return jnp.where(offset == index, factor, 0.0)
+
+        slope = at(-2, 1.0) + at(-1, -8.0) + at(1, 8.0) + at(2, -1.0)
+        bend = at(-2, -1.0) + at(-1, 16.0) + at(1, 16.0) + at(2, -1.0)
+        value = jnp.where(term == part, slope, jnp.where(term == part + 4, bend, 0.0))
+        i_matrix[...] = value.astype(jnp.bfloat16)
+
+    build_i()
 
     load_map.wait()
     load_links.wait()
@@ -313,6 +329,14 @@
 
         spread(value, delta_index, delta_mask, lower, upper, put)
 
+    def along_i():
+        piece = 2 * LANES
+        for part in range(width // piece):
+            at = slice(part * piece, (part + 1) * piece)
+            out = jnp.dot(i_matrix[...], split[:, at], preferred_element_type=jnp.float32)
+            slope_i[:, :, at] = out[:rows].reshape(4, length, piece)
+            bend_i[:, :, at] = out[rows:].reshape(3, length, piece)
+
     def along_k():
         count = 3 * length
         parts = []
@@ -407,20 +431,10 @@
             to_after.wait_send()
 
     lane = lax.broadcasted_iota(jnp.int32, (length, chunk), 1)
-    row_of = lax.broadcasted_iota(jnp.int32, (length, chunk), 0)
-
-    def central(value, minus2, minus1, plus1, plus2, bent):
+
+    def central(minus2, minus1, plus1, plus2, bent):
         slope = (minus2 - plus2) + 8.0 * (plus1 - minus1)
-        if not bent:
-            return slope, None
-        return slope, 16.0 * (minus1 + plus1) - (minus2 + plus2) - 30.0 * value
-
-    def along(value, bent):
-        def moved(step):
-            rolled = pltpu.roll(value, step % length, 0)
-            inside = row_of >= step if step > 0 else row_of < length + step
-            return jnp.where(inside, rolled, 0.0)
-        return central(value, moved(2), moved(1), moved(-1), moved(-2), bent)
+        return slope, 16.0 * (minus1 + plus1) - (minus2 + plus2) if bent else None
 
     def along_j(wide, value, wall, is_first, is_last, bent):
         def moved(step):
@@ -436,45 +450,48 @@
             p1 = jnp.where(lane >= chunk - cross, wall * value, plus1)
             p2 = jnp.where(lane >= chunk - cross, wall * minus1,
                            jnp.where(lane >= chunk - 2 * cross, wall * plus1, plus2))
-        return central(value, m2, m1, p1, p2, bent)
-
-    def rates_of(metric, values, slopes, bends):
-        carried = metric[0] * values[0] + metric[1] * values[1] + metric[2] * values[2]
-        norm = viscosity * (metric[0] * metric[0] + metric[1] * metric[1] + metric[2] * metric[2])
-        parts = [norm * bends[c] - carried * slopes[c] - metric[c] * slopes[3] for c in range(3)]
-        parts.append(-compress * (metric[0] * slopes[0] + metric[1] * slopes[1] + metric[2] * slopes[2]))
-        return parts
-
-    def inside_rates(padded, finish):
+        return central(m2, m1, p1, p2, bent)
+
+    def inside_rates(padded, fresh, finish):
         def at_chunk(start, is_first, is_last):
             at = pl.ds(start, chunk)
             wide = [padded[c, :, pl.ds(start, chunk + 2 * LANES)] for c in range(4)]
             values = [w[:, LANES:LANES + chunk] for w in wide]
-            sums = None
+            sums, total = None, None
             for direction in range(3):
                 metric = [geometry[3 * direction + b, :, at] for b in range(3)]
-                if direction == 2:
-                    slopes = [slope_k[c, :, at] for c in range(4)]
-                    bends = [bend_k[c, :, at] for c in range(3)]
-                else:
+                if direction == 1:
                     slopes, bends = [], []
                     for c in range(4):
-                        if direction == 0:
-                            slope, bend = along(values[c], c < 3)
-                        else:
-                            slope, bend = along_j(wide[c], values[c], WALL[c], is_first, is_last, c < 3)
+                        slope, bend = along_j(wide[c], values[c], WALL[c], is_first, is_last, c < 3)
                         slopes.append(slope)
                         bends.append(bend)
-                parts = rates_of(metric, values, slopes, bends)
+                else:
+                    slope_ref, bend_ref = (slope_i, bend_i) if direction == 0 else (slope_k, bend_k)
+                    slopes = [slope_ref[c, :, at] for c in range(4)]
+                    bends = [bend_ref[c, :, at] for c in range(3)]
+                if fresh:
+                    norm = viscosity * (metric[0] * metric[0] + metric[1] * metric[1] + metric[2] * metric[2])
+                    norms[direction, :, at] = norm
+                    total = norm if total is None else total + norm
+                else:
+                    norm = norms[direction, :, at]
+                carried = metric[0] * values[0] + metric[1] * values[1] + metric[2] * values[2]
+                parts = [norm * bends[c] - carried * slopes[c] - metric[c] * slopes[3] for c in range(3)]
+                parts.append(metric[0] * slopes[0] + metric[1] * slopes[1] + metric[2] * slopes[2])
                 sums = parts if sums is None else [a + b for a, b in zip(sums, parts)]
+            if fresh:
+                total = 30.0 * total
+                norms[3, :, at] = total
+            else:
+                total = norms[3, :, at]
             for c in range(4):
-                finish(c, start, values[c], sums[c])
+                finish(c, start, values[c], sums[c] - total * values[c] if c < 3 else sums[c])
 
         at_chunk(0, True, chunks == 1)
         if chunks > 2:
-            @pl.loop(1, chunks - 1)
-            def _(step):
-                at_chunk(pl.multiple_of(step * chunk, LANES), False, False)
+            for step in range(1, chunks - 1):
+                at_chunk(step * chunk, False, False)
         if chunks > 1:
             at_chunk((chunks - 1) * chunk, False, True)
 
@@ -541,12 +558,14 @@
 
     step_one, step_two = time_step / 12.0, 0.5 * time_step / 12.0
 
+    factor = (1.0, 1.0, 1.0, -compress)
+
     def finish_first(c, start, value, rate):
-        second[c, :, inside_second(start, chunk)] = value + step_one * rate
+        second[c, :, inside_second(start, chunk)] = value + (step_one * factor[c]) * rate
 
     def finish_second(c, start, value, rate):
         base = first[c, :, inside_second(start, chunk)]
-        out_ref[c, :, pl.ds(start, chunk)] = 0.5 * (base + value) + step_two * rate
+        out_ref[c, :, pl.ds(start, chunk)] = 0.5 * (base + value) + (step_two * factor[c]) * rate
 
     def read_second(c, which, start):
         return second[c, which, inside_second(start, chunk)]
@@ -588,8 +607,9 @@
     build_delta()
     prepare_terms(step_one, own_metric, face_out[0])
     split_up(first[:, :, inner].reshape(rows, width), split)
+    along_i()
     along_k()
-    inside_rates(first, finish_first)
+    inside_rates(first, True, finish_first)
 
     await_chain(0)
     chain_rates(first, 0, step_one, read_second, write_second, end_rows)
@@ -608,8 +628,9 @@
     spread_face(added, tile_second, put_second)
     open_ends(second, 1)
     split_up(second[:, :, inner].reshape(rows, width), split)
+    along_i()
     along_k()
-    inside_rates(second, finish_second)
+    inside_rates(second, False, finish_second)
     prepare_terms(step_two, face_out[1, :3 * length], added_ref[...])
     await_faces(1)
     their_face = received(0, rows)
@@ -655,8 +676,12 @@
             pltpu.VMEM((2 * chunk, chunk), bf16),
             pltpu.VMEM((2 * chunk, chunk), bf16),
             pltpu.VMEM((2 * chunk, chunk), bf16),
+            pltpu.VMEM((7 * length, LANES), bf16),
             pltpu.VMEM((parts, length, width), f32),
             pltpu.VMEM((parts - 1, length, width), f32),
+            pltpu.VMEM((parts, length, width), f32),
+            pltpu.VMEM((parts - 1, length, width), f32),
+            pltpu.VMEM((parts, length, width), f32),
             pltpu.VMEM((5, length, LANES), f32),
             pltpu.VMEM((parts * length, LANES), f32),
             pltpu.VMEM((parts * length, LANES), f32),

time: 13 us -> 12.4 us (0.954)
  Pallas kernels: 12 us -> 11.4 us
    pallas_call x1, Pallas kernels: 12 us -> 11.4 us  [on_device(): pl.pallas_call(functools.partial(kernel, segs, chain, cross), out_shape=p...]
where the time goes in v4:
time: 12.4 us; the launch traced here: 12.3 us
  Pallas kernels  11.4 us (92%)
  local copies, waits for them, and re-layouts  0.82 us (7%)
    pallas_call x1, Pallas kernels, on_device(): pl.pallas_call(functools.partial(kernel, segs, chain, cross), out_shape=p...  11.4 us
    unnamed x1, local copies, waits for them, and re-layouts  0.82 us

profile of v4, /device:TPU:1, one launch (start us, length us, event | category | flops | bytes accessed | tf_op | source)
XLA Modules:
  0.0 12.3 jit_solution(18216092327361738558)
XLA Ops:
  0.0 11.4 %shard_map.46 = f32[4,16,2304]{2,1,0:T(8,128)S(1)} custom-call(f32[1,4,16,2304]{3,2,1,0:T(8,128)} %state_hbm.1, f32[1,9,16,2304]{3,2,1,0:T(8,128)} %metric_hbm.1, s32[32]{0:T(128)} %block_map_hbm.1, s32[6,4,32]{2,1,0:T(4,128)} %bitcast.3), custom_call_target="tpu_custom_call" | custom-call | tf_op jit(solution)/shard_map/pallas_call | solution.py:662
  11.4 0.8 %copy.6 = f32[1,4,16,2304]{3,2,1,0:T(8,128)} copy(f32[1,4,16,2304]{3,2,1,0:T(8,128)S(1)} %bitcast.2) | data formatting | bytes 1179648

commit v5 on v4

--- a/solution.py
+++ b/solution.py
@@ -500,14 +500,14 @@
     row_sign = jnp.where(sub < 4, 1.0, -1.0)
 
     def chain_rates(padded, turn, scale, read, write, keep=None):
-        def body(step, carry):
-            start = pl.multiple_of(step * chunk, LANES)
+        for step in range(chunks):
+            start = step * chunk
             at = pl.ds(start, chunk)
 
             def ends(low, high):
                 return jnp.where(sub < 4, low, high)
 
-            inside = pl.ds(pl.multiple_of(start + LANES, LANES), chunk)
+            inside = pl.ds(start + LANES, chunk)
             values = [ends(padded[c, :8, inside], padded[c, length - 8:, inside]) for c in range(3)]
             metric = [ends(geometry[b, :8, at], geometry[b, length - 8:, at]) for b in range(3)]
             moved = [ghost_rows[turn, c, :, at] for c in range(4)]
@@ -521,9 +521,6 @@
                 write(c, high, start, high_new)
                 if keep is not None:
                     keep[c, :, at] = ends(low_new, high_new)
-            return carry
-
-        lax.fori_loop(0, chunks, body, 0)
 
     def at_part(value, c):
         return value[c * length:(c + 1) * length]

time: 12.4 us -> 12.2 us (0.984)
    pallas_call x1, Pallas kernels: 11.4 us -> 11.3 us  [on_device(): pl.pallas_call(functools.partial(kernel, segs, chain, cross), out_shape=p...]
where the time goes in v5:
time: 12.2 us; the launch traced here: 12.1 us
  Pallas kernels  11.3 us (93%)
  local copies, waits for them, and re-layouts  0.82 us (7%)
    pallas_call x1, Pallas kernels, on_device(): pl.pallas_call(functools.partial(kernel, segs, chain, cross), out_shape=p...  11.3 us
    unnamed x1, local copies, waits for them, and re-layouts  0.82 us

profile of v5, /device:TPU:1, one launch (start us, length us, event | category | flops | bytes accessed | tf_op | source)
XLA Modules:
  0.0 12.1 jit_solution(4448839744231873746)
XLA Ops:
  0.0 11.3 %shard_map.46 = f32[4,16,2304]{2,1,0:T(8,128)S(1)} custom-call(f32[1,4,16,2304]{3,2,1,0:T(8,128)} %state_hbm.1, f32[1,9,16,2304]{3,2,1,0:T(8,128)} %metric_hbm.1, s32[32]{0:T(128)} %block_map_hbm.1, s32[6,4,32]{2,1,0:T(4,128)} %bitcast.3), custom_call_target="tpu_custom_call" | custom-call | tf_op jit(solution)/shard_map/pallas_call | solution.py:659
  11.3 0.8 %copy.6 = f32[1,4,16,2304]{3,2,1,0:T(8,128)} copy(f32[1,4,16,2304]{3,2,1,0:T(8,128)S(1)} %bitcast.2) | data formatting | bytes 1179648

commit v6 on v5

--- a/solution.py
+++ b/solution.py
@@ -68,7 +68,7 @@
 
 
 def kernel(segs, chain, cross, state_hbm, metric_hbm, block_map_hbm, links_hbm, out_ref,
-           first, second, geometry, face_index, face_mask, delta_index, delta_mask, split,
+           first, second, geometry, face_index, face_mask, delta_index, delta_mask, face_hot, split,
            k_slope_uvw, k_slope_p, k_bend, i_matrix, slope_k, bend_k, slope_i, bend_i, norms,
            terms_ref, added_ref, theirs_ref, turned_ref,
            ghost_rows, end_rows, delta_out, delta_in, face_out, face_in, block_map, links,
@@ -205,6 +205,9 @@
     place_of = lane_of - HALF * layer_of
     face_lane = place_of < cross
 
+    tiles = width // LANES
+    split_tile = tiles // 4 * 2
+
     def spread_index(tile, high):
         start = tile * LANES
         row = start // cross
@@ -227,6 +230,14 @@
         build_spread(face_index, face_mask, jnp.full((8, LANES), select(on_high, 1, 0)) > 0,
                      jnp.full((8, LANES), select(on_second, 1, 0)) > 0)
 
+        cells = lax.broadcasted_iota(jnp.int32, (2 * LANES, LANES), 0)
+        source = jnp.where(face_lane, source_of, -1)[0:1]
+        source = source - (1 - select(on_second, 1, 0)) * (2 * width)
+        for piece in range((tiles - split_tile) // 2):
+            start = (split_tile + 2 * piece) * LANES
+            hit = (cells == source - start).astype(jnp.float32).astype(jnp.bfloat16)
+            face_hot[piece * 2 * LANES:(piece + 1) * 2 * LANES, :] = hit
+
     def build_delta():
         def chosen(sides):
             flags = [select(jnp.logical_or(near_joins[sides[0]], near_joins[sides[1]]), 1, 0)
@@ -257,9 +268,9 @@
         into[:count] = lead
         into[count:2 * count] = trail
 
-    def gathered(low, high, tile_of):
-        packed = None
-        for tile in range(width // LANES):
+    def gathered(low, high, tile_of, rest=None):
+        packed = None if rest is None else rest
+        for tile in range(tiles if rest is None else split_tile):
             part = by_rows(tile_of(tile), lambda x: take(x, source_lane, 1))
             here = jnp.concatenate([source_tile == tile] * (part.shape[0] // 8), axis=0)
             packed = part if packed is None else jnp.where(here, part, packed)
@@ -268,12 +279,17 @@
         upper = jnp.where(lane_row < HALF, pltpu.roll(high, LANES - near, 1), pltpu.roll(high, HALF - far, 1))
         return jnp.where(on_first, jnp.where(on_high, upper, lower), packed)
 
-    def gather_face(padded):
+    def gather_face(padded, shared):
         def tile_of(tile):
             start = LANES + tile * LANES
             return padded[:, :, start:start + LANES].reshape(rows, LANES)
 
-        return gathered(tile_of(0), tile_of(width // LANES - 1), tile_of)
+        if not shared:
+            return gathered(tile_of(0), tile_of(tiles - 1), tile_of)
+        value = padded[:, :, LANES + split_tile * LANES:LANES + width].reshape(rows, (tiles - split_tile) * LANES)
+        both = jnp.concatenate(halves(value), axis=0)
+        rest = jnp.dot(both, face_hot[...], preferred_element_type=jnp.float32)
+        return gathered(tile_of(0), tile_of(tiles - 1), tile_of, rest[:rows] + rest[rows:])
 
     def gather_metric():
         def tile_of(tile, base=6):
@@ -289,8 +305,19 @@
     def to_upper(value):
         return jnp.where(lane_row >= near, pltpu.roll(value, near, 1), pltpu.roll(value, LANES - (HALF - far), 1))
 
-    def spread(value, index_ref, mask_ref, lower, upper, write):
-        for tile in range(width // LANES):
+    def spread(value, index_ref, mask_ref, lower, upper, write, shared):
+        last = split_tile if shared else tiles
+        if shared:
+            both = jnp.concatenate(halves(value), axis=0)
+            for piece in range((tiles - last) // 2):
+                add = lax.dot_general(both, face_hot[piece * 2 * LANES:(piece + 1) * 2 * LANES, :],
+                                      (((1,), (1,)), ((), ())), preferred_element_type=jnp.float32)
+                add = add[:rows] + add[rows:]
+                for side in range(2):
+                    tile = last + 2 * piece + side
+                    part = add[:, side * LANES:(side + 1) * LANES]
+                    write(tile * LANES, part + upper if tile == tiles - 1 else part)
+        for tile in range(last):
             index, mask = index_ref[tile], mask_ref[tile]
             add = by_rows(value, lambda x: take(x, index, 1) * mask)
             if tile == 0:
@@ -308,7 +335,7 @@
             for c in range(4):
                 write(c, start, read(c, start) + add[c * length:(c + 1) * length])
 
-        spread(value, face_index, face_mask, lower, upper, put)
+        spread(value, face_index, face_mask, lower, upper, put, True)
 
     def spread_delta():
         end_row = lax.broadcasted_iota(jnp.int32, (8, LANES), 0)
@@ -327,7 +354,7 @@
                 at = slice(start, start + LANES)
                 ghost_rows[1, c, :, at] = ghost_rows[1, c, :, at] + add[c * 8:(c + 1) * 8]
 
-        spread(value, delta_index, delta_mask, lower, upper, put)
+        spread(value, delta_index, delta_mask, lower, upper, put, False)
 
     def along_i():
         piece = 2 * LANES
@@ -589,7 +616,7 @@
         out_ref[c, :, start:start + LANES] = value
 
     load_state.wait()
-    face_out[0] = gather_face(first)
+    face_out[0] = gather_face(first, False)
     pl.semaphore_wait(barrier, segs - 1 + has_before.astype(jnp.int32) + has_after.astype(jnp.int32))
     start_faces(0)
     start_chain(0)
@@ -611,7 +638,7 @@
     await_chain(0)
     chain_rates(first, 0, step_one, read_second, write_second, end_rows)
     start_chain(1)
-    face_out[2] = gather_face(second)
+    face_out[2] = gather_face(second, False)
     start_faces(2)
 
     turned_ref[...] = flipped(face_out[0])
@@ -638,14 +665,13 @@
     await_chain(2)
     spread_delta()
     chain_rates(second, 1, step_two, read_out, write_out)
-    await_faces(2)
-    their_face = flipped(received(2, rows) + theirs_ref[...])
-    spread_face(face_rates(own_terms(), their_face, added_ref[...]), tile_out, put_out)
-
     for kind in range(3):
         for copy in face_copies(kind):
             copy.wait_send()
         sent_chain(kind)
+    await_faces(2)
+    their_face = flipped(received(2, rows) + theirs_ref[...])
+    spread_face(face_rates(own_terms(), their_face, added_ref[...]), tile_out, put_out)
 
 
 def on_device(state, metric, block_map, links):
@@ -669,6 +695,7 @@
             pltpu.VMEM((width // LANES, 8, LANES), f32),
             pltpu.VMEM((width // LANES, 8, LANES), jnp.int32),
             pltpu.VMEM((width // LANES, 8, LANES), f32),
+            pltpu.VMEM((width - width // LANES // 4 * 2 * LANES, LANES), bf16),
             pltpu.VMEM((2 * parts * length, width), bf16),
             pltpu.VMEM((2 * chunk, chunk), bf16),
             pltpu.VMEM((2 * chunk, chunk), bf16),

time: 12.2 us -> 12.1 us (level)
  no operation moved by 1% of the time
where the time goes in v6:
time: 12.1 us; the launch traced here: 12 us
  Pallas kernels  11.2 us (93%)
  local copies, waits for them, and re-layouts  0.82 us (7%)
    pallas_call x1, Pallas kernels, on_device(): pl.pallas_call(functools.partial(kernel, segs, chain, cross), out_shape=p...  11.2 us
    unnamed x1, local copies, waits for them, and re-layouts  0.82 us

profile of v6, /device:TPU:1, one launch (start us, length us, event | category | flops | bytes accessed | tf_op | source)
XLA Modules:
  0.0 12.0 jit_solution(12654093798463480212)
XLA Ops:
  0.0 11.2 %shard_map.46 = f32[4,16,2304]{2,1,0:T(8,128)S(1)} custom-call(f32[1,4,16,2304]{3,2,1,0:T(8,128)} %state_hbm.1, f32[1,9,16,2304]{3,2,1,0:T(8,128)} %metric_hbm.1, s32[32]{0:T(128)} %block_map_hbm.1, s32[6,4,32]{2,1,0:T(4,128)} %bitcast.3), custom_call_target="tpu_custom_call" | custom-call | tf_op jit(solution)/shard_map/pallas_call | solution.py:685
  11.2 0.8 %copy.6 = f32[1,4,16,2304]{3,2,1,0:T(8,128)} copy(f32[1,4,16,2304]{3,2,1,0:T(8,128)S(1)} %bitcast.2) | data formatting | bytes 1179648

commit v7 on v6

--- a/solution.py
+++ b/solution.py
@@ -206,7 +206,7 @@
     face_lane = place_of < cross
 
     tiles = width // LANES
-    split_tile = tiles // 4 * 2
+    split_tile = tiles // 6 * 2
 
     def spread_index(tile, high):
         start = tile * LANES
@@ -572,8 +572,10 @@
             value = jnp.where(comes_from[offset], face_in[kind, offset - 1, :count], value)
         return value
 
-    def face_rates(terms, theirs, own):
-        ghosts = [at_part(theirs, c) - WALL[c] * at_part(own, c) for c in range(4)]
+    def face_rates(terms, theirs, own=None):
+        ghosts = [at_part(theirs, c) for c in range(4)]
+        if own is not None:
+            ghosts = [g - WALL[c] * at_part(own, c) for c, g in enumerate(ghosts)]
         moved = [pltpu.roll(g, HALF, 1) for g in ghosts]
         return jnp.concatenate(ghost_rates(near_lane, terms, ghosts, moved), axis=0)
 
@@ -641,7 +643,6 @@
     face_out[2] = gather_face(second, False)
     start_faces(2)
 
-    turned_ref[...] = flipped(face_out[0])
     await_faces(0)
     added = face_rates(own_terms(), flipped(received(0, rows)), face_out[0])
     for c in range(4):
@@ -659,7 +660,9 @@
     await_faces(1)
     their_face = received(0, rows)
     their_terms = terms_of(step_one, partner_sign, received(1, 3 * length), their_face)
-    theirs_ref[...] = face_rates(their_terms, turned_ref[...], their_face)
+    theirs = flipped(face_rates(their_terms, flipped(face_out[0]), their_face))
+    for c in range(4):
+        theirs_ref[c * length:(c + 1) * length] = at_part(theirs, c) - WALL[c] * at_part(added_ref[...], c)
 
     await_chain(1)
     await_chain(2)
@@ -670,8 +673,8 @@
             copy.wait_send()
         sent_chain(kind)
     await_faces(2)
-    their_face = flipped(received(2, rows) + theirs_ref[...])
-    spread_face(face_rates(own_terms(), their_face, added_ref[...]), tile_out, put_out)
+    their_face = flipped(received(2, rows)) + theirs_ref[...]
+    spread_face(face_rates(own_terms(), their_face), tile_out, put_out)
 
 
 def on_device(state, metric, block_map, links):
@@ -695,7 +698,7 @@
             pltpu.VMEM((width // LANES, 8, LANES), f32),
             pltpu.VMEM((width // LANES, 8, LANES), jnp.int32),
             pltpu.VMEM((width // LANES, 8, LANES), f32),
-            pltpu.VMEM((width - width // LANES // 4 * 2 * LANES, LANES), bf16),
+            pltpu.VMEM((width - width // LANES // 6 * 2 * LANES, LANES), bf16),
             pltpu.VMEM((2 * parts * length, width), bf16),
             pltpu.VMEM((2 * chunk, chunk), bf16),
             pltpu.VMEM((2 * chunk, chunk), bf16),

time: 12.1 us -> 12.1 us (level)
  no operation moved by 1% of the time
where the time goes in v7:
time: 12.1 us; the launch traced here: 12 us
  Pallas kernels  11.2 us (93%)
  local copies, waits for them, and re-layouts  0.82 us (7%)
    pallas_call x1, Pallas kernels, on_device(): pl.pallas_call(functools.partial(kernel, segs, chain, cross), out_shape=p...  11.2 us
    unnamed x1, local copies, waits for them, and re-layouts  0.82 us

profile of v7, /device:TPU:1, one launch (start us, length us, event | category | flops | bytes accessed | tf_op | source)
XLA Modules:
  0.0 12.0 jit_solution(9377431752371618586)
XLA Ops:
  0.0 11.2 %shard_map.46 = f32[4,16,2304]{2,1,0:T(8,128)S(1)} custom-call(f32[1,4,16,2304]{3,2,1,0:T(8,128)} %state_hbm.1, f32[1,9,16,2304]{3,2,1,0:T(8,128)} %metric_hbm.1, s32[32]{0:T(128)} %block_map_hbm.1, s32[6,4,32]{2,1,0:T(4,128)} %bitcast.3), custom_call_target="tpu_custom_call" | custom-call | tf_op jit(solution)/shard_map/pallas_call | solution.py:688
  11.2 0.8 %copy.6 = f32[1,4,16,2304]{3,2,1,0:T(8,128)} copy(f32[1,4,16,2304]{3,2,1,0:T(8,128)S(1)} %bitcast.2) | data formatting | bytes 1179648
